TPU v7x, 32 devices: a whole 2x2x4 slice. The times are simulated.
32 devices in a mesh: rep: 2 (over x), ga: 16 (over z, y, core).
Axes of the slice: x: 2, y: 2, z: 4, core: 2. Of those that a mesh axis runs over, the one named last changes fastest.
Arguments:
- positions: float32 [64, 3, 768], P('rep', None, 'ga'), parts along dimension 0, may hold values from -3 to 23, as said below
- weights: int32 [1, 32], replicated, may hold values from 1 to 16
- psi: bfloat16 [2, 512, 2, 32768], P('rep', None, None, 'ga'), parts along dimension 0, may hold values from -5 to 5
- vloc: float32 [2, 32768], P('rep'), parts along dimension 0, may hold values from -8 to 8
Outputs:
- psi_new: bfloat16 [2, 512, 2, 32768], P('rep', None, None, 'ga'), parts along dimension 0
- bead_forces: float32 [64, 3, 768], P('rep', None, 'ga'), parts along dimension 0
There are 2 independent parts, one for each index of `rep`. A program takes and returns all parts, laid end to end along the dimension named above; an argument that names none is the same for every part. Nothing has to cross between parts.
Inputs may be any that keep to these rules, and one draw needn't show every extreme that they name: `positions`: atom 3w is the oxygen of water w and atoms 3w+1 and 3w+2 are its hydrogens; in every bead each hydrogen lies between 1.0 and 2.6 from its oxygen.
All inputs are finite; a program needn't handle non-finite values.
Results may differ from a plain program's by a relative error of at most 0.0037.
The roundings to bfloat16 on the way count: a program that leaves them out, or rounds other values in their place, can miss the bound.
Values may be sent and summed in bfloat16 or wider, within the bound.
A program may use at most 192 MiB of HBM per device.

v0:
```python
import jax
import jax.numpy as jnp
from jax import lax
from jax.sharding import PartitionSpec as P

BEADS = 32
CBEADS = 1
WATERS = 256
NGRID = 32
GVECS = 32768


box_length = 20.0
bond_stiff = 0.5
bond_rest = 1.8
spring_stiff = 2.0
width_square = 0.09
step_size = 0.02
nonlocal_strength = 250.0
occupation = 2.0
highest = lax.Precision.HIGHEST


def frequency(index, count):
    signed = jnp.where(index < count // 2, index, index - count)
    return signed.astype(jnp.float32) * (2.0 * jnp.pi / box_length)


def field_forces(positions):
    oxygen = positions[:, :, 0::3]
    toward_one = positions[:, :, 1::3] - oxygen
    toward_two = positions[:, :, 2::3] - oxygen

    def stretch(offset):
        length = jnp.sqrt(jnp.sum(offset * offset, axis=1, keepdims=True))
        return -bond_stiff * (length - bond_rest) * offset / length

    pull_one = stretch(toward_one)
    pull_two = stretch(toward_two)
    bonds = jnp.stack([-(pull_one + pull_two), pull_one, pull_two], axis=3).reshape(positions.shape)
    springs = 2.0 * positions - jnp.roll(positions, 1, axis=0) - jnp.roll(positions, -1, axis=0)
    return bonds - spring_stiff * springs


def inner(left_mat, right_mat):
    return lax.dot_general(
        left_mat, right_mat, (((1,), (1,)), ((), ())), preferred_element_type=jnp.float32
    )


def real_form(freq_index, group_index):
    product = freq_index[:, None] * freq_index[None, :] % NGRID
    angle = product.astype(jnp.float32) * (2.0 * jnp.pi / NGRID)
    same = (group_index[:, None] == group_index[None, :]).astype(jnp.float32)
    cosines = jnp.cos(angle) * same
    sines = jnp.sin(angle) * same
    return jnp.stack([jnp.stack([cosines, sines], 1), jnp.stack([-sines, cosines], 1)], 0)


def plane_table():
    index = jnp.arange(NGRID, dtype=jnp.int32)
    return real_form(index, jnp.zeros_like(index))


def block_table(length, within):
    index = jnp.arange(length, dtype=jnp.int32)
    if within:
        return real_form(index % NGRID, index // NGRID)
    return real_form(index // NGRID, index % NGRID)


def per_device(positions, weights, psi, vloc):
    near_forces = field_forces(positions)
    weight_float = weights.astype(jnp.float32)
    mixing = weight_float / jnp.sum(weight_float, axis=1, keepdims=True)
    centres = jnp.einsum("cj,jan->can", mixing, positions, precision=highest)
    everyone = lax.all_gather(centres, "ga", axis=2, tiled=True)
    parts = lax.axis_size("ga")
    bands = psi.shape[1]
    local_g = psi.shape[3]
    flat_index = lax.axis_index("ga") * local_g + jnp.arange(local_g, dtype=jnp.int32)
    gvectors = jnp.stack(
        [
            frequency(flat_index // (NGRID * NGRID), NGRID),
            frequency(flat_index // NGRID % NGRID, NGRID),
            frequency(flat_index % NGRID, NGRID),
        ]
    )
    square = jnp.sum(gvectors * gvectors, axis=0)
    profile = jnp.exp(-0.5 * width_square * square)
    kinetic = 0.5 * square
    x_table = plane_table()
    y_table = block_table(NGRID * NGRID, False)
    z_table = block_table(local_g, True)
    oxygens = everyone[0][:, 0::3]
    phases = jnp.einsum("ai,ag->ig", oxygens, gvectors, precision=highest)
    wave_cos = profile * jnp.cos(phases)
    wave_sin = profile * jnp.sin(phases)
    table = jnp.concatenate(
        [jnp.concatenate([wave_cos, -wave_sin], 1), jnp.concatenate([wave_sin, wave_cos], 1)], 0
    ).astype(jnp.bfloat16)
    wavefunc = psi[0].reshape(bands, 2 * local_g)
    real_part = wavefunc[:, :local_g]
    imag_part = wavefunc[:, local_g:]
    partial_proj = (inner(table, wavefunc) * (1.0 / GVECS)).reshape(2, WATERS, bands)
    share = lax.psum_scatter(partial_proj, "ga", scatter_dimension=1, tiled=True).astype(
        jnp.bfloat16
    )
    paired = jnp.concatenate([wavefunc, jnp.concatenate([imag_part, -real_part], 1)], 0).reshape(
        2, bands, 2 * local_g
    )
    table_blocks = table.reshape(2, WATERS, 2 * local_g)
    all_proj = lax.all_gather(share, "ga", axis=1, tiled=True)
    nonlocal_term = jnp.einsum(
        "kib,kig->bg", all_proj, table_blocks, preferred_element_type=jnp.float32
    )
    weighted = jnp.einsum("kib,kbg->ig", all_proj, paired, preferred_element_type=jnp.float32)
    mixed_wave = wave_cos * weighted[:, local_g:] + wave_sin * weighted[:, :local_g]
    force_part = (
        2.0
        * occupation
        * nonlocal_strength
        / GVECS
        * jnp.einsum("ag,ig->ai", gvectors, mixed_wave, precision=highest)
    )
    oxygen_force = lax.psum_scatter(force_part, "ga", scatter_dimension=1, tiled=True)
    hydrogen_zero = jnp.zeros_like(oxygen_force)
    dft_forces = [jnp.stack([oxygen_force, hydrogen_zero, hydrogen_zero], axis=2).reshape(3, -1)]
    wave_float = psi[0].astype(jnp.float32)
    grid_potential = vloc[0].reshape(1, 1, NGRID, NGRID * NGRID)
    grouped_raw = psi[0].reshape(parts, bands // parts, 2, local_g)
    planes = lax.all_to_all(grouped_raw, "ga", split_axis=0, concat_axis=3, tiled=True)
    band_count = planes.shape[1]
    blocks_whole = planes.astype(jnp.float32).reshape(band_count, 2, NGRID**3 // local_g, local_g)
    along_z = jnp.einsum("mckp,cpdq->mdkq", blocks_whole, z_table, precision=highest) * (
        1.0 / NGRID
    )
    grid = along_z.reshape(band_count, 2, NGRID, NGRID * NGRID)
    grid = jnp.einsum("mcxr,cxdw->mdwr", grid, x_table, precision=highest) * (1.0 / NGRID)
    grid = jnp.einsum("mcxp,cpdq->mdxq", grid, y_table, precision=highest) * (1.0 / NGRID)
    grid = grid * grid_potential
    grid = jnp.einsum("mdxq,cpdq->mcxp", grid, y_table, precision=highest)
    grid = jnp.einsum("mdwr,cxdw->mcxr", grid, x_table, precision=highest)
    returning = grid.reshape(1, band_count, 2, NGRID**3)
    returned = lax.all_to_all(
        returning.astype(jnp.bfloat16), "ga", split_axis=3, concat_axis=0, tiled=True
    ).astype(returning.dtype)
    returned = returned.reshape(bands, 2, local_g)
    potential = jnp.einsum("bdq,cpdq->bcp", returned, z_table, precision=highest)
    hamil_re = (
        kinetic * wave_float[:, 0]
        + potential[:, 0]
        + nonlocal_strength * nonlocal_term[:, :local_g]
    )
    hamil_im = (
        kinetic * wave_float[:, 1]
        + potential[:, 1]
        + nonlocal_strength * nonlocal_term[:, local_g:]
    )
    trial = jnp.concatenate(
        [wave_float[:, 0] - step_size * hamil_re, wave_float[:, 1] - step_size * hamil_im], 1
    ).astype(jnp.bfloat16)
    rotated = jnp.concatenate(
        [trial, jnp.concatenate([-trial[:, local_g:], trial[:, :local_g]], 1)], 0
    )
    margin = lax.psum(inner(trial, rotated) * (1.0 / GVECS), "ga")
    identity_rows = jnp.concatenate(
        [jnp.eye(bands, dtype=jnp.float32), jnp.zeros((bands, bands), jnp.float32)], 1
    )
    mixer = (1.5 * identity_rows - 0.5 * margin).astype(jnp.bfloat16)
    updated = jnp.dot(mixer, rotated, preferred_element_type=jnp.float32)
    new_waves = [updated.astype(jnp.bfloat16).reshape(bands, 2, local_g)]
    contracted_force = jnp.einsum("cj,can->jan", mixing, jnp.stack(dft_forces), precision=highest)
    bead_forces = near_forces + BEADS / CBEADS * contracted_force
    return (jnp.stack(new_waves), bead_forces)


def solution(mesh):
    placed = (P("rep", None, "ga"), P(), P("rep", None, None, "ga"), P("rep", None))
    return jax.shard_map(
        per_device,
        mesh=mesh,
        in_specs=placed,
        out_specs=(P("rep", None, None, "ga"), P("rep", None, "ga")),
        check_vma=False,
    )
```

profile of v0, /device:TPU:0, one launch (start us, length us, event | category | flops | bytes accessed | tf_op | source)
XLA Modules:
  0.0 955.4 jit_solution(13431449668949625740)
XLA Ops:
  7.2 6.1 copy.56
  13.3 7.7 all-to-all-start
  21.6 17.4 %compare_select_fusion.2 = (f32[1024,1,1024]{2,0,1:T(8,128)S(1)}, f32[1024,1,1024]{2,0,1:T(8,128)S(1)}, f32[1024,1,1024]{2,0,1:T(8,128)S(1)}) fusion(s32[1024]{0:T(1024)S(1)} %get-tuple-element.51, s32[1024]{0:T(1024)S(1)} %get-tuple-element.52), kind=kLoop, calls=%fused_computation.48 | loop fusion | flops 18874368 | bytes 12591104 | tf_op jit(solution)/shard_map/mul | solution.py:56
  39.0 6.8 maximum_bitcast_fusion.2
  45.7 70.9 %compare_select_fusion = (f32[2048,1,2048]{2,0,1:T(8,128)S(1)}, f32[2048,1,2048]{2,0,1:T(8,128)}, f32[2048,1,2048]{2,0,1:T(8,128)}) fusion(s32[2048]{0:T(1024)S(1)} %get-tuple-element.53, s32[2048]{0:T(1024)S(1)} %get-tuple-element.54), kind=kLoop, calls=%fused_computation.11 | loop fusion | flops 75497472 | bytes 50348032 | tf_op jit(solution)/shard_map/mul | solution.py:56
  116.6 38.3 %maximum_bitcast_fusion = (f32[1,2048,2,2048]{3,1,0,2:T(8,128)}, f32[1,2048,2,2048]{3,1,0,2:T(8,128)}) fusion(f32[2048,1,2048]{2,0,1:T(8,128)S(1)} %get-tuple-element.37, f32[2048,1,2048]{2,0,1:T(8,128)} %get-tuple-element.39, f32[2048,1,2048]{2,0,1:T(8,128)} %get-tuple-element.38), kind=kLoop, calls=%fused_computation.4 | loop fusion | flops 16777216 | bytes 117440512 | tf_op jit(solution)/shard_map/stack | solution.py:57
  155.0 59.7 %fusion.17 = f32[32,2,16,2048]{3,0,2,1:T(8,128)S(1)} fusion(f32[1,2048,2,2048]{3,1,0,2:T(8,128)} %get-tuple-element.17, f32[1,2048,2,2048]{3,1,0,2:T(8,128)} %get-tuple-element.16, bf16[16,32,2,2048]{3,1,2,0:T(8,128)(2,1)} %all-to-all-done), kind=kOutput, calls=%fused_computation.37 | convolution fusion | flops 103098089472 | bytes 79691776 | tf_op jit(solution)/shard_map/mckp,cpdq->mdkq/dot_general | solution.py:135
  214.7 8.2 copy.57
  222.8 9.4 reshape.1000
  232.2 11.9 %fusion.16 = f32[32,2,32,1024]{3,2,0,1:T(8,128)} fusion(f32[32,2,32,1024,1]{3,2,1,0,4:T(8,128)} %reshape.1000, f32[1,32,2,32]{1,3,0,2:T(8,128)S(1)} %get-tuple-element.36, f32[1,32,2,32]{1,3,0,2:T(8,128)S(1)} %get-tuple-element.35), kind=kOutput, calls=%fused_computation.35 | convolution fusion | flops 1612713984 | bytes 16793600 | tf_op jit(solution)/shard_map/mcxr,cxdw->mdwr/dot_general | solution.py:139
  244.1 78.9 %fusion.13 = f32[32,2,32,1024,1]{3,0,2,1,4:T(8,128)} fusion(f32[32,1024]{1,0:T(8,128)S(1)} %mul.488, f32[32,2,32,1024]{3,2,0,1:T(8,128)} %fusion.16, f32[1,1024,2,1024]{3,1,0,2:T(8,128)} %get-tuple-element.21, f32[1,1024,2,1024]{3,1,0,2:T(8,128)} %get-tuple-element.20), kind=kOutput, calls=%fused_computation.30 | convolution fusion | flops 51545899008 | bytes 33685504 | tf_op jit(solution)/shard_map/mcxp,cpdq->mdxq/dot_general | solution.py:140
  323.0 72.7 %fusion.8 = f32[2,1024,32,32,1]{1,3,4,0,2:T(8,128)} fusion(f32[32,2,32,1024,1]{3,0,2,1,4:T(8,128)} %fusion.13, f32[1,1024,2,1024]{3,1,0,2:T(8,128)S(1)} %bitcast.215, f32[1,1024,2,1024]{3,1,0,2:T(8,128)S(1)} %bitcast.213), kind=kOutput, calls=%fused_computation.19 | convolution fusion | flops 51543801856 | bytes 33554432 | tf_op jit(solution)/shard_map/mdxq,cpdq->mcxp/dot_general | solution.py:142
  395.8 10.3 %fusion.26 = bf16[32,2,32,1024]{3,2,0,1:T(8,128)(2,1)} fusion(f32[2,1024,32,32,1]{1,3,4,0,2:T(8,128)} %fusion.8, f32[1,32,2,32]{1,3,0,2:T(8,128)S(1)} %get-tuple-element.36, f32[1,32,2,32]{1,3,0,2:T(8,128)S(1)} %get-tuple-element.35), kind=kOutput, calls=%fused_computation.54 | convolution fusion | flops 1612713984 | bytes 12599296 | tf_op jit(solution)/shard_map/mdwr,cxdw->mcxr/dot_general | solution.py:143
  406.1 26.3 %copy.92 = bf16[32,2,32,1024]{0,1,3,2:T(2,128)(2,1)} copy(bf16[32,2,32,1024]{3,2,0,1:T(8,128)(2,1)} %fusion.26) | data formatting | bytes 8388608 | tf_op jit(solution)/shard_map/convert_element_type | solution.py:146
  432.4 20.7 %reshape.1027 = bf16[16,2,65536]{2,1,0:T(2,128)(2,1)} reshape(bf16[32768,1,2,32]{3,2,1,0:T(2,128)(2,1)} %bitcast.203) | data formatting | bytes 8388608
  453.1 6.3 all-to-all-start.1
  460.9 82.9 %all-gather.1 = f32[16,48,3]{1,2,0:T(4,128)S(1)} all-gather(f32[1,48,3]{1,2,0:T(4,128)S(1)} %bitcast.220), channel_id=2, replica_groups=mesh['rep'=2,'ga'=16] {'ga'}, dimensions={0}, use_global_device_ids=true | all-gather | bytes 9792 | tf_op jit(solution)/shard_map/all_gather | solution.py:77
  544.0 6.6 copy.96
  550.9 9.9 %cosine_multiply_fusion = (f32[256,2048]{1,0:T(8,128)}, f32[256,2048]{1,0:T(8,128)S(1)}) fusion(f32[2048]{0:T(1024)S(1)} %get-tuple-element.41, f32[3,256]{1,0:T(4,128)S(1)} %slice.68, f32[1,2048]{1,0:T(1,128)S(1)} %fusion.86, f32[1,2048]{1,0:T(1,128)S(1)} %get-tuple-element.50, f32[1,2048]{1,0:T(1,128)S(1)} %get-tuple-element.49), kind=kOutput, calls=%fused_computation.84 | convolution fusion | flops 19410944 | bytes 4230144 | tf_op jit(solution)/shard_map/ai,ag->ig/dot_general | solution.py:96
  560.7 7.6 fusion.116
  583.5 21.5 %maximum_maximum_fusion.1 = bf16[1024,4096]{1,0:T(8,128)(2,1)} fusion(bf16[512,2048]{1,0:T(8,128)(2,1)S(1)} %get-tuple-element.19, bf16[512,2048]{1,0:T(8,128)(2,1)S(1)} %get-tuple-element.18, bf16[512,4096]{1,0:T(8,128)(2,1)S(1)} %bitcast.209), kind=kLoop, calls=%fused_computation.26 | loop fusion | flops 25165824 | bytes 16777216 | tf_op jit(solution)/shard_map/concatenate | solution.py:109
  610.2 44.4 %reduce-scatter.5.cloned.1.call-done = f32[2,16,512]{2,1,0:T(8,128)} async-done(((f32[2,256,512]{2,1,0:T(8,128)}), f32[2,16,512]{2,1,0:T(8,128)}) %reduce-scatter.5.cloned.1.call-update) | async-done | bytes 65552 | tf_op jit(solution)/shard_map/reduce_scatter | solution.py:106
  655.6 20.8 %all_gather.7 = bf16[2,256,512]{2,1,0:T(8,128)(2,1)S(1)} all-gather(bf16[2,16,512]{2,1,0:T(8,128)(2,1)S(1)} %convert_element_type.163), channel_id=1, replica_groups=mesh['rep'=2,'ga'=16] {'ga'}, dimensions={1}, use_global_device_ids=true | all-gather | bytes 557056 | tf_op jit(solution)/shard_map/all_gather | solution.py:113
  685.1 7.9 convolution_bitcast_fusion
  693.0 16.1 %reshape.1028 = bf16[32768,1,2,32]{3,2,1,0:T(2,128)(2,1)} reshape(bf16[16,2,65536]{2,1,0:T(2,128)(2,1)} %all-to-all-done.1) | data formatting | bytes 8388608
  709.1 38.1 %copy.63 = bf16[1,32,2,16,2048]{4,1,3,2,0:T(8,128)(2,1)} copy(bf16[1,32,2,16,2048]{1,2,4,3,0:T(2,128)(2,1)} %bitcast.204) | data formatting | bytes 8388608 | tf_op jit(solution)/shard_map/all_to_all | solution.py:145
  747.1 59.1 %fusion.20 = f32[512,2,2048]{2,0,1:T(8,128)S(1)} fusion(bf16[512,2,2048,1]{2,0,3,1:T(8,128)(2,1)} %bitcast.216, f32[1,2048,2,2048]{3,1,0,2:T(8,128)} %get-tuple-element.17, f32[1,2048,2,2048]{3,1,0,2:T(8,128)} %get-tuple-element.16), kind=kOutput, calls=%fused_computation.50 | convolution fusion | flops 103095992320 | bytes 79691776 | tf_op jit(solution)/shard_map/bdq,cpdq->bcp/dot_general | solution.py:149
  810.8 6.5 fusion.35
  817.4 5.9 broadcast_multiply_fusion
  826.4 92.2 %all-reduce.4.cloned.1.call-done = f32[512,1024]{1,0:T(8,128)} async-done(((f32[512,1024]{1,0:T(8,128)}), f32[512,1024]{1,0:T(8,128)}) %all-reduce.4.cloned.1.call-update) | async-done | bytes 2097168 | tf_op jit(solution)/shard_map/psum | solution.py:166
  918.6 22.2 %convolution_convert_fusion = bf16[512,4096]{1,0:T(8,128)(2,1)} fusion(bf16[512,2048]{1,0:T(8,128)(2,1)S(1)} %fusion.35, bf16[512,2048]{1,0:T(8,128)(2,1)} %copy-done.4, bf16[512,2048]{1,0:T(8,128)(2,1)} %copy-done.5, f32[512,1024]{1,0:T(8,128)} %all-reduce.4.cloned.1.call-done, pred[512,512]{1,0:T(32,128)(4,1)S(1)} %iota_compare_fusion), kind=kOutput, calls=%fused_computation.45 | convolution fusion | flops 4332716032 | bytes 12845056 | tf_op jit(solution)/shard_map/dot_general | solution.py:171
  940.9 7.8 stack_reshape.4
  (85 shorter events, 40.1 us)
Async XLA Ops:
  7.2 13.8 %copy-start.7 = (f32[1,32768]{1,0:T(1,128)S(1)}, f32[1,32768]{1,0:T(1,128)}, u32[]{:S(2)}) copy-start(f32[1,32768]{1,0:T(1,128)} %param.7) | copy-start | bytes 393220
  13.3 141.7 %all-to-all-start = ((bf16[16,32,2,2048]{3,1,2,0:T(8,128)(2,1)}), bf16[16,32,2,2048]{3,1,2,0:T(8,128)(2,1)}, u32[]{:S(2)}, u32[]{:S(2)}) async-start(bf16[16,32,2,2048]{3,1,2,0:T(8,128)(2,1)} %copy.56), calls=%async_computation | async-start | bytes 8388608 | tf_op jit(solution)/shard_map/all_to_all | solution.py:132
  232.2 90.8 %slice-start = ((s8[8388608]{0:T(1024)(128)(4,1)}), s8[4194304]{0:T(1024)(128)(4,1)S(1)}, s32[]{:S(2)}) async-start(s8[8388608]{0:T(1024)(128)(4,1)} %bitcast.212), calls=%async_computation.7 | async-start | bytes 8388608
  232.2 90.8 %slice-start.2 = ((s8[8388608]{0:T(1024)(128)(4,1)}), s8[4194304]{0:T(1024)(128)(4,1)S(1)}, s32[]{:S(2)}) async-start(s8[8388608]{0:T(1024)(128)(4,1)} %bitcast.214), calls=%async_computation.9 | async-start | bytes 8388608
  244.1 78.9 %slice-start.1 = ((s8[8388608]{0:T(1024)(128)(4,1)}), s8[4194304]{0:T(1024)(128)(4,1)S(1)}, s32[]{:S(2)}) async-start(s8[8388608]{0:T(1024)(128)(4,1)} %bitcast.212), calls=%async_computation.8 | async-start | bytes 8388608
  244.1 78.9 %slice-start.3 = ((s8[8388608]{0:T(1024)(128)(4,1)}), s8[4194304]{0:T(1024)(128)(4,1)S(1)}, s32[]{:S(2)}) async-start(s8[8388608]{0:T(1024)(128)(4,1)} %bitcast.214), calls=%async_computation.10 | async-start | bytes 8388608
  453.1 6.3 copy-start.8
  453.1 7.0 copy-start.6
  453.1 239.8 %all-to-all-start.1 = ((bf16[16,2,65536]{2,1,0:T(2,128)(2,1)}), bf16[16,2,65536]{2,1,0:T(2,128)(2,1)}, u32[]{:S(2)}, u32[]{:S(2)}) async-start(bf16[16,2,65536]{2,1,0:T(2,128)(2,1)} %reshape.1027), calls=%async_computation.1 | async-start | bytes 8388608 | tf_op jit(solution)/shard_map/all_to_all | solution.py:145
  459.4 195.2 %reduce-scatter.5.cloned.1.call-start = ((), (), s32[]{:S(2)}) async-start(), calls=%async_computation.4 | async-start | bytes 1114112 | tf_op jit(solution)/shard_map/reduce_scatter | solution.py:106
  560.7 12.8 %copy-start.1 = (bf16[64,8,2,2048]{3,1,2,0:T(8,128)(2,1)S(1)}, bf16[64,8,2,2048]{3,1,2,0:T(8,128)(2,1)}, u32[]{:S(2)}) copy-start(bf16[64,8,2,2048]{3,1,2,0:T(8,128)(2,1)} %copy.96) | copy-start | bytes 12582916
  579.2 245.4 %reduce-scatter.7.cloned.1.call-start = ((), (), s32[]{:S(2)}) async-start(), calls=%async_computation.6 | async-start | bytes 139264
  580.0 3.5 copy-start.2
  583.5 21.5 %copy-start = (bf16[1,512,2,2048]{3,2,1,0:T(2,128)(2,1)S(1)}, bf16[1,512,2,2048]{3,2,1,0:T(2,128)(2,1)}, u32[]{:S(2)}) copy-start(bf16[1,512,2,2048]{3,2,1,0:T(2,128)(2,1)} %param.6) | copy-start | bytes 12582916
  654.6 27.6 %copy-start.3 = (f32[256,2048]{1,0:T(8,128)S(1)}, f32[256,2048]{1,0:T(8,128)}, u32[]{:S(2)}) copy-start(f32[256,2048]{1,0:T(8,128)} %get-tuple-element.45) | copy-start | bytes 6291460
  684.8 233.8 %all-reduce.4.cloned.1.call-start = ((), (), s32[]{:S(2)}) async-start(), calls=%async_computation.5 | async-start | bytes 4194304 | tf_op jit(solution)/shard_map/psum | solution.py:166
  810.8 6.6 copy-start.4
  810.8 6.6 copy-start.5
Sparse Core Ops, SparseCore 0:
  579.3 75.2 reduce-scatter.4
  685.0 52.8 reduce-scatter.6
  823.4 95.2 all-reduce.3
where the time goes:
time: 961 us; the launch traced here: 955 us
  matrix products  352 us (37%)
  other arithmetic  190 us (20%)
  local copies, waits for them, and re-layouts  144 us (15%)
  waiting for transfers between devices  137 us (14%)
  blocking collectives  104 us (11%)
  between operations  14.4 us (1%)
  starting transfers between devices  14.2 us (1%)
    psum x1, waiting for transfers between devices, per_device(): margin = lax.psum(inner(trial, rotated) * (1.0 / GVECS), 'ga')  92.2 us
    mul x2, other arithmetic, real_form(): sines = jnp.sin(angle) * same  88.3 us
    all_gather x1, blocking collectives, per_device(): everyone = lax.all_gather(centres, 'ga', axis=2, tiled=True)  82.9 us
    dot_general x1, matrix products, per_device(): jnp.einsum('mcxp,cpdq->mdxq', grid, y_table, precision=highest)  78.9 us
    dot_general x1, matrix products, per_device(): grid = jnp.einsum('mdxq,cpdq->mcxp', grid, y_table, precision=highest)  72.7 us
    dot_general x1, matrix products, per_device(): jnp.einsum('mckp,cpdq->mdkq', blocks_whole, z_table, precision=highest)  59.7 us
    dot_general x1, matrix products, per_device(): jnp.einsum('bdq,cpdq->bcp', returned, z_table, precision=highest)  59.1 us
    unnamed x35, local copies, waits for them, and re-layouts  46.7 us
  transfers between devices with their start and end apart: 5, of which 2 were waited for; matrix products, arithmetic and copies ran while one was open for 37% of the time, Pallas kernels for 0%

commit v1 on v0

--- a/solution.py
+++ b/solution.py
@@ -1,5 +1,6 @@
 import jax
 import jax.numpy as jnp
+import numpy as np
 from jax import lax
 from jax.sharding import PartitionSpec as P
 
@@ -8,6 +9,7 @@
 WATERS = 256
 NGRID = 32
 GVECS = 32768
+CHUNKS = 2
 
 
 box_length = 20.0
@@ -67,6 +69,132 @@
     if within:
         return real_form(index % NGRID, index // NGRID)
     return real_form(index // NGRID, index % NGRID)
+
+
+def grid_sum(psi, vloc, parts):
+    bands = psi.shape[1]
+    local_g = psi.shape[3]
+    x_table = plane_table()
+    z_table = block_table(local_g, True)
+    y_table = block_table(NGRID * NGRID, False)
+    grid_potential = vloc[0].reshape(1, 1, NGRID, NGRID * NGRID)
+    grouped_raw = psi[0].reshape(parts, bands // parts, 2, local_g)
+    planes = lax.all_to_all(grouped_raw, "ga", split_axis=0, concat_axis=3, tiled=True)
+    band_count = planes.shape[1]
+    blocks_whole = planes.astype(jnp.float32).reshape(band_count, 2, NGRID**3 // local_g, local_g)
+    along_z = jnp.einsum("mckp,cpdq->mdkq", blocks_whole, z_table, precision=highest) * (
+        1.0 / NGRID
+    )
+    grid = along_z.reshape(band_count, 2, NGRID, NGRID * NGRID)
+    grid = jnp.einsum("mcxr,cxdw->mdwr", grid, x_table, precision=highest) * (1.0 / NGRID)
+    grid = jnp.einsum("mcxp,cpdq->mdxq", grid, y_table, precision=highest) * (1.0 / NGRID)
+    grid = grid * grid_potential
+    grid = jnp.einsum("mdxq,cpdq->mcxp", grid, y_table, precision=highest)
+    grid = jnp.einsum("mdwr,cxdw->mcxr", grid, x_table, precision=highest)
+    returning = grid.reshape(1, band_count, 2, NGRID**3)
+    returned = lax.all_to_all(
+        returning.astype(jnp.bfloat16), "ga", split_axis=3, concat_axis=0, tiled=True
+    ).astype(returning.dtype)
+    returned = returned.reshape(bands, 2, local_g)
+    potential = jnp.einsum("bdq,cpdq->bcp", returned, z_table, precision=highest)
+    return potential[:, 0], potential[:, 1]
+
+
+def plane_rotation():
+    small = np.arange(NGRID)
+    angle = small[:, None] * small[None, :] % NGRID * (2.0 * np.pi / NGRID)
+    side = NGRID * NGRID
+    wave = np.kron(np.exp(1j * angle), np.exp(1j * angle))
+    real, imag = np.real(wave), np.imag(wave)
+    table = np.stack([np.stack([real, -imag], 1), np.stack([imag, real], 1)], 1)
+    return jnp.asarray(table.reshape(2 * side, 2 * side).astype(np.float32), jnp.bfloat16)
+
+
+def line_rotation(group):
+    small = np.arange(NGRID)
+    angle = small[:, None] * small[None, :] % NGRID * (2.0 * np.pi / NGRID)
+    real, imag = np.cos(angle), np.sin(angle)
+    form = np.stack([np.stack([real, -imag], 2), np.stack([imag, real], 2)], 1)
+    same = np.eye(group)
+    table = form[:, None, :, :, None, :] * same[None, :, None, None, :, None]
+    size = 2 * NGRID * group
+    return jnp.asarray(table.reshape(size, size).astype(np.float32), jnp.bfloat16)
+
+
+def plane_sum(psi, vloc, parts):
+    bands = psi.shape[1]
+    local_g = psi.shape[3]
+    side = NGRID * NGRID
+    planes = local_g // side
+    points = side // parts
+    group = min(8, points)
+    groups = points // group
+    chunk = bands // CHUNKS
+    plane_table = plane_rotation()
+    line_table = line_rotation(group)
+    start = lax.axis_index("ga") * points
+    own = lax.dynamic_slice_in_dim(vloc[0].reshape(NGRID, side), start, points, axis=1)
+    own = own.reshape(NGRID, groups, group).transpose(1, 0, 2) * (1.0 / (NGRID * side))
+    own = jnp.broadcast_to(own[..., None], (groups, NGRID, group, 2)).reshape(groups, -1, 1)
+    scaled = (own * line_table.astype(jnp.float32)).astype(jnp.bfloat16)
+    action = jnp.einsum(
+        "ea,gec->gac", line_table, scaled, preferred_element_type=jnp.float32
+    ).astype(jnp.bfloat16)
+    reals, imags = [], []
+    for first in range(0, bands, chunk):
+        part = psi[0, first : first + chunk].reshape(chunk, 2, planes, side)
+        part = part.transpose(2, 0, 1, 3).reshape(planes, chunk, 2 * side)
+        sent = jnp.stack(
+            [
+                jnp.einsum(
+                    "qk,bk->qb", plane_table, part[p], preferred_element_type=jnp.float32
+                )
+                .astype(jnp.bfloat16)
+                .reshape(parts, 2 * points, chunk)
+                for p in range(planes)
+            ],
+            1,
+        )
+        lines = lax.all_to_all(sent, "ga", split_axis=0, concat_axis=0, tiled=True)
+        lines = lines.reshape(parts * planes, groups, 2 * group, chunk)
+        lines = lines.transpose(1, 0, 2, 3).reshape(groups, -1, chunk)
+        lines = jnp.einsum(
+            "gac,gcb->gab", action, lines, preferred_element_type=jnp.float32
+        ).astype(jnp.bfloat16)
+        lines = lines.reshape(groups, parts * planes, 2 * group, chunk).transpose(1, 0, 2, 3)
+        lines = lines.reshape(parts, planes, 2 * points, chunk)
+        back = lax.all_to_all(lines, "ga", split_axis=0, concat_axis=0, tiled=True)
+        whole = [
+            jnp.einsum(
+                "qb,qk->bk",
+                back[:, p].reshape(2 * side, chunk),
+                plane_table,
+                preferred_element_type=jnp.float32,
+            )
+            for p in range(planes)
+        ]
+        reals.append(jnp.concatenate([w[:, :side] for w in whole], 1))
+        imags.append(jnp.concatenate([w[:, side:] for w in whole], 1))
+    return jnp.concatenate(reals, 0), jnp.concatenate(imags, 0)
+
+
+def waves(oxygens, gvectors, profile):
+    local_g = profile.shape[0]
+    side = NGRID * NGRID
+    if local_g % side:
+        phases = jnp.einsum("ai,ag->ig", oxygens, gvectors, precision=highest)
+        return profile * jnp.cos(phases), profile * jnp.sin(phases)
+    spots = oxygens.T
+    flat = spots[:, 1:2] * gvectors[1:2, :side] + spots[:, 2:3] * gvectors[2:3, :side]
+    flat_cos, flat_sin = jnp.cos(flat), jnp.sin(flat)
+    along = spots[:, 0:1] * gvectors[0:1, ::side]
+    along_cos, along_sin = jnp.cos(along), jnp.sin(along)
+    cosines, sines = [], []
+    for p in range(local_g // side):
+        c, s = along_cos[:, p : p + 1], along_sin[:, p : p + 1]
+        cosines.append(c * flat_cos - s * flat_sin)
+        sines.append(s * flat_cos + c * flat_sin)
+    return profile * jnp.concatenate(cosines, 1), profile * jnp.concatenate(sines, 1)
 
 
 def per_device(positions, weights, psi, vloc):
@@ -89,13 +217,8 @@
     square = jnp.sum(gvectors * gvectors, axis=0)
     profile = jnp.exp(-0.5 * width_square * square)
     kinetic = 0.5 * square
-    x_table = plane_table()
-    y_table = block_table(NGRID * NGRID, False)
-    z_table = block_table(local_g, True)
     oxygens = everyone[0][:, 0::3]
-    phases = jnp.einsum("ai,ag->ig", oxygens, gvectors, precision=highest)
-    wave_cos = profile * jnp.cos(phases)
-    wave_sin = profile * jnp.sin(phases)
+    wave_cos, wave_sin = waves(oxygens, gvectors, profile)
     table = jnp.concatenate(
         [jnp.concatenate([wave_cos, -wave_sin], 1), jnp.concatenate([wave_sin, wave_cos], 1)], 0
     ).astype(jnp.bfloat16)
@@ -127,34 +250,18 @@
     hydrogen_zero = jnp.zeros_like(oxygen_force)
     dft_forces = [jnp.stack([oxygen_force, hydrogen_zero, hydrogen_zero], axis=2).reshape(3, -1)]
     wave_float = psi[0].astype(jnp.float32)
-    grid_potential = vloc[0].reshape(1, 1, NGRID, NGRID * NGRID)
-    grouped_raw = psi[0].reshape(parts, bands // parts, 2, local_g)
-    planes = lax.all_to_all(grouped_raw, "ga", split_axis=0, concat_axis=3, tiled=True)
-    band_count = planes.shape[1]
-    blocks_whole = planes.astype(jnp.float32).reshape(band_count, 2, NGRID**3 // local_g, local_g)
-    along_z = jnp.einsum("mckp,cpdq->mdkq", blocks_whole, z_table, precision=highest) * (
-        1.0 / NGRID
-    )
-    grid = along_z.reshape(band_count, 2, NGRID, NGRID * NGRID)
-    grid = jnp.einsum("mcxr,cxdw->mdwr", grid, x_table, precision=highest) * (1.0 / NGRID)
-    grid = jnp.einsum("mcxp,cpdq->mdxq", grid, y_table, precision=highest) * (1.0 / NGRID)
-    grid = grid * grid_potential
-    grid = jnp.einsum("mdxq,cpdq->mcxp", grid, y_table, precision=highest)
-    grid = jnp.einsum("mdwr,cxdw->mcxr", grid, x_table, precision=highest)
-    returning = grid.reshape(1, band_count, 2, NGRID**3)
-    returned = lax.all_to_all(
-        returning.astype(jnp.bfloat16), "ga", split_axis=3, concat_axis=0, tiled=True
-    ).astype(returning.dtype)
-    returned = returned.reshape(bands, 2, local_g)
-    potential = jnp.einsum("bdq,cpdq->bcp", returned, z_table, precision=highest)
+    if local_g % (NGRID * NGRID) == 0 and (NGRID * NGRID) % parts == 0:
+        potential = plane_sum(psi, vloc, parts)
+    else:
+        potential = grid_sum(psi, vloc, parts)
     hamil_re = (
         kinetic * wave_float[:, 0]
-        + potential[:, 0]
+        + potential[0]
         + nonlocal_strength * nonlocal_term[:, :local_g]
     )
     hamil_im = (
         kinetic * wave_float[:, 1]
-        + potential[:, 1]
+        + potential[1]
         + nonlocal_strength * nonlocal_term[:, local_g:]
     )
     trial = jnp.concatenate(
@@ -163,11 +270,15 @@
     rotated = jnp.concatenate(
         [trial, jnp.concatenate([-trial[:, local_g:], trial[:, :local_g]], 1)], 0
     )
-    margin = lax.psum(inner(trial, rotated) * (1.0 / GVECS), "ga")
-    identity_rows = jnp.concatenate(
-        [jnp.eye(bands, dtype=jnp.float32), jnp.zeros((bands, bands), jnp.float32)], 1
-    )
-    mixer = (1.5 * identity_rows - 0.5 * margin).astype(jnp.bfloat16)
+    row = lax.broadcasted_iota(jnp.int32, (bands, bands), 0)
+    column = lax.broadcasted_iota(jnp.int32, (bands, bands), 1)
+    both = inner(trial, rotated) * (1.0 / GVECS)
+    packed = lax.psum(jnp.where(row <= column, both[:, :bands], both[:, bands:]), "ga")
+    turned = packed.T
+    even = jnp.where(row <= column, packed, turned)
+    odd = jnp.where(row > column, packed, jnp.where(row < column, -turned, 0.0))
+    identity = (row == column).astype(jnp.float32)
+    mixer = jnp.concatenate([1.5 * identity - 0.5 * even, -0.5 * odd], 1).astype(jnp.bfloat16)
     updated = jnp.dot(mixer, rotated, preferred_element_type=jnp.float32)
     new_waves = [updated.astype(jnp.bfloat16).reshape(bands, 2, local_g)]
     contracted_force = jnp.einsum("cj,can->jan", mixing, jnp.stack(dft_forces), precision=highest)

time: 961 us -> 493 us (0.51)
  matrix products: 352 us -> 90 us
  other arithmetic: 190 us -> 65.6 us
  local copies, waits for them, and re-layouts: 144 us -> 52 us
  starting transfers between devices: 14.2 us -> 38.1 us
  blocking collectives: 104 us -> 84.7 us
    dot_general x7 -> x11, matrix products: 302 us -> 41.2 us  [the longest x4 17.9 us: plane_sum(): jnp.einsum('qb,qk->bk', back[:, p].reshape(2 * side, chunk), plane_table,...]
    mul x3 -> x2, other arithmetic: 88.6 us -> 1.72 us  [the longest x1 1.63 us: waves(): profile * jnp.concatenate(cosines, 1)]
    another operation x4, other arithmetic: 45.8 us -> 5.22 us  [the longest x2 3.04 us: plane_sum(): jnp.stack([jnp.einsum('qk,bk->qb', plane_table, part[p], preferred_elemen...]
    all_to_all x1 -> x0, local copies, waits for them, and re-layouts: 38.1 us -> none  [per_device(): lax.all_to_all(returning.astype(jnp.bfloat16), 'ga', split_axis=3, concat...]
    all_gather x1, blocking collectives: 82.9 us -> 50.4 us  [per_device(): everyone = lax.all_gather(centres, 'ga', axis=2, tiled=True)]
    unnamed x35 -> x64, local copies, waits for them, and re-layouts: 46.7 us -> 20.1 us
    convert_element_type x1 -> x0, local copies, waits for them, and re-layouts: 26.3 us -> none  [per_device(): returning.astype(jnp.bfloat16)]
    all_to_all x2 -> x4, starting transfers between devices: 13.9 us -> 37.6 us  [the longest x2 19 us: plane_sum(): back = lax.all_to_all(lines, 'ga', split_axis=0, concat_axis=0, tiled=True)]
  transfers between devices with their start and end apart: 5 -> 7, of which waited for: 2 -> 3; matrix products, arithmetic and copies ran while one was open for 37% -> 31% of each run, Pallas kernels for 0% -> 0%
where the time goes in v1:
time: 493 us; the launch traced here: 484 us
  waiting for transfers between devices  139 us (28%)
  matrix products  90 us (18%)
  blocking collectives  84.7 us (17%)
  other arithmetic  65.6 us (13%)
  local copies, waits for them, and re-layouts  52 us (11%)
  starting transfers between devices  38.1 us (8%)
  between operations  14.9 us (3%)
    psum x1, waiting for transfers between devices, per_device(): lax.psum(jnp.where(row <= column, both[:, :bands], both[:, bands:]), 'ga')  94.7 us
    all_gather x1, blocking collectives, per_device(): everyone = lax.all_gather(centres, 'ga', axis=2, tiled=True)  50.4 us
    all_gather x1, blocking collectives, per_device(): all_proj = lax.all_gather(share, 'ga', axis=1, tiled=True)  34.4 us
    reduce_scatter x1, waiting for transfers between devices, per_device(): lax.psum_scatter(partial_proj, 'ga', scatter_dimension=1, tiled=True)  22.6 us
    all_to_all x2, waiting for transfers between devices, plane_sum(): lines = lax.all_to_all(sent, 'ga', split_axis=0, concat_axis=0, tiled=True)  21.7 us
    dot_general x1, matrix products, per_device(): updated = jnp.dot(mixer, rotated, preferred_element_type=jnp.float32)  21.6 us
    concatenate x1, other arithmetic, per_device(): jnp.concatenate([wavefunc, jnp.concatenate([imag_part, -real_part], 1)], 0)  21.4 us
    unnamed x64, local copies, waits for them, and re-layouts  20.1 us
  transfers between devices with their start and end apart: 7, of which 3 were waited for; matrix products, arithmetic and copies ran while one was open for 31% of the time, Pallas kernels for 0%

profile of v1, /device:TPU:0, one launch (start us, length us, event | category | flops | bytes accessed | tf_op | source)
XLA Modules:
  0.0 484.2 jit_solution(8314571569704070288)
XLA Ops:
  7.2 6.0 %fusion.61 = (bf16[1,256,2,2048]{3,2,1,0:T(2,128)(2,1)}, bf16[1,256,2,2048]{3,2,1,0:T(2,128)(2,1)}) fusion(bf16[1,512,2,2048]{3,2,1,0:T(2,128)(2,1)} %param.8), kind=kLoop, calls=%fused_computation.130 | loop fusion | bytes 8388608 | tf_op jit(solution)/shard_map/slice | solution.py:145
  13.2 4.7 copy.92
  18.0 5.9 %convolution_convert_fusion.4 = bf16[2048,256]{1,0:T(8,128)(2,1)S(1)} fusion(bf16[2048,2048]{1,0:T(8,128)(2,1)} %constant.99.clone, bf16[256,2048]{0,1:T(8,128)(2,1)S(1)} %bitcast.187), kind=kOutput, calls=%fused_computation.33 | convolution fusion | flops 2148007936 | bytes 10485760 | tf_op jit(solution)/shard_map/qk,bk->qb/dot_general | solution.py:149
  23.9 2.5 convolution_convert_fusion.3
  28.0 7.4 %all-to-all-start = ((bf16[16,2,128,256]{3,2,1,0:T(8,128)(2,1)}), bf16[16,2,128,256]{3,2,1,0:T(8,128)(2,1)S(1)}, u32[]{:S(2)}, u32[]{:S(2)}) async-start(bf16[16,2,128,256]{3,2,1,0:T(8,128)(2,1)} %pad_maximum_fusion), calls=%async_computation | async-start | bytes 4194304 | tf_op jit(solution)/shard_map/all_to_all | solution.py:158
  36.8 6.1 %copy.93 = bf16[1,256,2,2048]{1,3,2,0:T(8,128)(2,1)} copy(bf16[1,256,2,2048]{3,2,1,0:T(2,128)(2,1)} %get-tuple-element.19) | data formatting | bytes 4194304
  44.8 5.9 %convolution_convert_fusion.2 = bf16[2048,256]{1,0:T(8,128)(2,1)S(1)} fusion(bf16[2048,2048]{1,0:T(8,128)(2,1)} %constant.99.clone, bf16[256,2048]{0,1:T(8,128)(2,1)S(1)} %bitcast.188), kind=kOutput, calls=%fused_computation.31 | convolution fusion | flops 2148007936 | bytes 10485760 | tf_op jit(solution)/shard_map/qk,bk->qb/dot_general | solution.py:149
  54.7 21.7 %all-to-all-done = bf16[16,2,128,256]{3,2,1,0:T(8,128)(2,1)S(1)} async-done(((bf16[16,2,128,256]{3,2,1,0:T(8,128)(2,1)}), bf16[16,2,128,256]{3,2,1,0:T(8,128)(2,1)S(1)}, u32[]{:S(2)}, u32[]{:S(2)}) %all-to-all-start) | async-done | bytes 2097184 | tf_op jit(solution)/shard_map/all_to_all | solution.py:158
  76.4 11.3 %all-to-all-start.2 = ((bf16[16,2,128,256]{3,2,1,0:T(8,128)(2,1)}), bf16[16,2,128,256]{3,2,1,0:T(8,128)(2,1)}, u32[]{:S(2)}, u32[]{:S(2)}) async-start(bf16[16,2,128,256]{3,2,1,0:T(8,128)(2,1)} %pad_maximum_fusion.1), calls=%async_computation.2 | async-start | bytes 4194304 | tf_op jit(solution)/shard_map/all_to_all | solution.py:158
  88.0 50.4 %all-gather.1 = f32[16,48,3]{1,2,0:T(4,128)S(1)} all-gather(f32[1,48,3]{1,2,0:T(4,128)S(1)} %bitcast.197), channel_id=2, replica_groups=mesh['rep'=2,'ga'=16] {'ga'}, dimensions={0}, use_global_device_ids=true | all-gather | bytes 9792 | tf_op jit(solution)/shard_map/all_gather | solution.py:205
  140.9 4.2 multiply_add_fusion.1
  145.1 3.6 fusion.15
  155.2 11.2 %all-to-all-start.1 = ((bf16[16,2,128,256]{3,2,1,0:T(8,128)(2,1)}), bf16[16,2,128,256]{3,2,1,0:T(8,128)(2,1)}, u32[]{:S(2)}, u32[]{:S(2)}) async-start(bf16[16,2,128,256]{3,2,1,0:T(8,128)(2,1)} %bitcast.170), calls=%async_computation.1 | async-start | bytes 4194304 | tf_op jit(solution)/shard_map/all_to_all | solution.py:166
  166.7 5.3 %maximum_convert_fusion = bf16[512,4096]{1,0:T(8,128)(2,1)} fusion(f32[256,2048]{1,0:T(8,128)} %maximum_multiply_fusion, f32[256,2048]{1,0:T(8,128)S(1)} %get-tuple-element.15, bf16[256,2048]{1,0:T(8,128)(2,1)} %get-tuple-element.14), kind=kLoop, calls=%fused_computation | loop fusion | flops 16777216 | bytes 9437184 | tf_op jit(solution)/shard_map/convert_element_type | solution.py:224
  174.5 3.3 convolution_multiply_fusion
  178.8 2.6 fusion.60
  182.2 5.4 %bitcast_convert_fusion = f32[512,2,2048]{2,0,1:T(8,128)} fusion(bf16[1,512,2,2048]{3,2,1,0:T(2,128)(2,1)S(1)} %copy-done.1), kind=kLoop, calls=%fused_computation.26 | loop fusion | flops 2097152 | bytes 12582912 | tf_op jit(solution)/shard_map/convert_element_type | solution.py:252
  187.6 21.4 %maximum_maximum_fusion.1 = bf16[1024,4096]{1,0:T(8,128)(2,1)} fusion(bf16[512,2048]{1,0:T(8,128)(2,1)S(1)} %get-tuple-element.17, bf16[512,2048]{1,0:T(8,128)(2,1)S(1)} %get-tuple-element.16, bf16[512,4096]{1,0:T(8,128)(2,1)S(1)} %bitcast.163), kind=kLoop, calls=%fused_computation.2 | loop fusion | flops 25165824 | bytes 16777216 | tf_op jit(solution)/shard_map/concatenate | solution.py:232
  214.9 7.8 %all-to-all-start.3 = ((bf16[16,2,128,256]{3,2,1,0:T(8,128)(2,1)}), bf16[16,2,128,256]{3,2,1,0:T(8,128)(2,1)}, u32[]{:S(2)}, u32[]{:S(2)}) async-start(bf16[16,2,128,256]{3,2,1,0:T(8,128)(2,1)} %bitcast.169), calls=%async_computation.3 | async-start | bytes 4194304 | tf_op jit(solution)/shard_map/all_to_all | solution.py:166
  223.5 22.6 %reduce-scatter.5.cloned.1.call-done = f32[2,16,512]{2,1,0:T(8,128)} async-done(((f32[2,256,512]{2,1,0:T(8,128)}), f32[2,16,512]{2,1,0:T(8,128)}) %reduce-scatter.5.cloned.1.call-update) | async-done | bytes 65552 | tf_op jit(solution)/shard_map/reduce_scatter | solution.py:229
  246.9 34.4 %all_gather.7 = bf16[2,256,512]{2,1,0:T(8,128)(2,1)S(1)} all-gather(bf16[2,16,512]{2,1,0:T(8,128)(2,1)S(1)} %convert_element_type.99), channel_id=1, replica_groups=mesh['rep'=2,'ga'=16] {'ga'}, dimensions={1}, use_global_device_ids=true | all-gather | bytes 557056 | tf_op jit(solution)/shard_map/all_gather | solution.py:236
  281.3 5.9 %convolution_bitcast_fusion.1 = f32[256,4096]{1,0:T(8,128)S(1)} fusion(bf16[2,256,512]{2,1,0:T(8,128)(2,1)S(1)} %all_gather.7, bf16[2,512,4096]{2,1,0:T(8,128)(2,1)} %bitcast.166), kind=kOutput, calls=%fused_computation.6 | convolution fusion | flops 2147483648 | bytes 13107200 | tf_op jit(solution)/shard_map/kib,kbg->ig/dot_general | solution.py:240
  290.1 7.8 %convolution_bitcast_fusion = f32[512,4096]{1,0:T(8,128)} fusion(bf16[2,256,512]{2,1,0:T(8,128)(2,1)S(1)} %all_gather.7, bf16[2,256,4096]{2,1,0:T(8,128)(2,1)} %bitcast.167), kind=kOutput, calls=%fused_computation.4 | convolution fusion | flops 2147483648 | bytes 13107200 | tf_op jit(solution)/shard_map/kib,kig->bg/dot_general | solution.py:237
  299.8 5.9 %fusion.76 = f32[256,2048]{1,0:T(8,128)S(1)} fusion(bf16[2048,256]{1,0:T(8,128)(2,1)S(1)} %bitcast.179, bf16[2048,2048]{1,0:T(8,128)(2,1)} %constant.99.clone), kind=kOutput, calls=%fused_computation.145 | convolution fusion | flops 2147483648 | bytes 11534336 | tf_op jit(solution)/shard_map/qb,qk->bk/dot_general | solution.py:168
  305.8 3.7 fusion.75
  311.4 5.9 %fusion.78 = f32[256,2048]{1,0:T(8,128)S(1)} fusion(bf16[2048,256]{1,0:T(8,128)(2,1)S(1)} %bitcast.180, bf16[2048,2048]{1,0:T(8,128)(2,1)} %constant.99.clone), kind=kOutput, calls=%fused_computation.147 | convolution fusion | flops 2147483648 | bytes 11534336 | tf_op jit(solution)/shard_map/qb,qk->bk/dot_general | solution.py:168
  324.9 6.4 %fusion.8 = bf16[512,2048]{1,0:T(8,128)(2,1)} fusion(f32[512,4096]{1,0:T(8,128)} %convolution_bitcast_fusion, f32[256,1024]{1,0:T(8,128)S(1)} %get-tuple-element.74, f32[256,1024]{1,0:T(8,128)S(1)} %get-tuple-element.27, f32[256,1024]{1,0:T(8,128)S(1)} %get-tuple-element.72, f32[256,1024]{1,0:T(8,128)S(1)} %get-tuple-element.23, ...), kind=kLoop, calls=%fused_computation.18 | loop fusion | flops 10485760 | bytes 14688256 | tf_op jit(solution)/shard_map/slice | solution.py:271
  331.3 7.8 %fusion.57 = (bf16[512,2048]{1,0:T(8,128)(2,1)S(1)}, bf16[512,2048]{1,0:T(8,128)(2,1)}) fusion(f32[512,4096]{1,0:T(8,128)} %convolution_bitcast_fusion, f32[256,1024]{1,0:T(8,128)} %get-tuple-element.75, f32[256,1024]{1,0:T(8,128)} %get-tuple-element.26, f32[256,1024]{1,0:T(8,128)} %get-tuple-element.73, f32[256,1024]{1,0:T(8,128)} %get-tuple-element.22, ...), kind=kLoop, calls=%fused_computation.127 | loop fusion | flops 11534336 | bytes 16785408 | tf_op jit(solution)/shard_map/neg | solution.py:271
  339.1 7.5 %broadcast_multiply_fusion = f32[512,1024]{1,0:T(8,128)S(1)} fusion(bf16[512,2048]{1,0:T(8,128)(2,1)S(1)} %copy-done.11, bf16[512,2048]{1,0:T(8,128)(2,1)S(1)} %get-tuple-element.12, bf16[512,2048]{1,0:T(8,128)(2,1)} %get-tuple-element.13), kind=kOutput, calls=%fused_computation.62 | convolution fusion | flops 4337434624 | bytes 8388608 | tf_op jit(solution)/shard_map/dot_general | solution.py:48
  350.1 94.7 %all-reduce.3.cloned.1.call-done = f32[512,512]{1,0:T(8,128)} async-done(((f32[512,512]{1,0:T(8,128)}), f32[512,512]{1,0:T(8,128)}) %all-reduce.3.cloned.1.call-update) | async-done | bytes 1048592 | tf_op jit(solution)/shard_map/psum | solution.py:276
  447.9 21.6 %convolution_convert_fusion = bf16[512,4096]{1,0:T(8,128)(2,1)} fusion(bf16[512,2048]{1,0:T(8,128)(2,1)S(1)} %copy-done.11, bf16[512,2048]{1,0:T(8,128)(2,1)} %copy-done.12, bf16[512,2048]{1,0:T(8,128)(2,1)} %get-tuple-element.13, bf16[512,512]{1,0:T(8,128)(2,1)S(1)} %get-tuple-element.21, bf16[512,512]{1,0:T(8,128)(2,1)S(1)} %get-tuple-element.20), kind=kOutput, calls=%fused_computation.5 | convolution fusion | flops 4332716032 | bytes 11534336 | tf_op jit(solution)/shard_map/dot_general | solution.py:282
  469.5 7.8 %stack_reshape.20 = bf16[1,512,2,2048]{3,2,1,0:T(2,128)(2,1)} reshape(bf16[512,4096]{1,0:T(8,128)(2,1)} %convolution_convert_fusion) | data formatting | bytes 8388608 | tf_op jit(solution)/shard_map/stack;reshape | solution.py:286
  (140 shorter events, 50.9 us)
Async XLA Ops:
  17.8 6.1 %slice-start = ((s8[8388608]{0:T(1024)(128)(4,1)}), s8[4194304]{0:T(1024)(128)(4,1)S(1)}, s32[]{:S(2)}) async-start(s8[8388608]{0:T(1024)(128)(4,1)} %bitcast.152), calls=%async_computation.9 | async-start | bytes 8388608
  18.0 5.9 %slice-start.1 = ((s8[8388608]{0:T(1024)(128)(4,1)}), s8[4194304]{0:T(1024)(128)(4,1)S(1)}, s32[]{:S(2)}) async-start(s8[8388608]{0:T(1024)(128)(4,1)} %bitcast.152), calls=%async_computation.10 | async-start | bytes 8388608
  26.4 9.0 %copy-start.15 = (s32[1,32]{1,0:T(1,128)S(1)}, s32[1,32]{1,0:T(1,128)}, u32[]{:S(2)}) copy-start(s32[1,32]{1,0:T(1,128)} %param.7) | copy-start | bytes 388
  26.4 9.6 %copy-start.13 = (f32[32,3,48]{2,0,1:T(8,128)S(1)}, f32[32,3,48]{2,0,1:T(8,128)}, u32[]{:S(2)}) copy-start(f32[32,3,48]{2,0,1:T(8,128)} %param.6) | copy-start | bytes 55300
  28.0 48.4 %all-to-all-start = ((bf16[16,2,128,256]{3,2,1,0:T(8,128)(2,1)}), bf16[16,2,128,256]{3,2,1,0:T(8,128)(2,1)S(1)}, u32[]{:S(2)}, u32[]{:S(2)}) async-start(bf16[16,2,128,256]{3,2,1,0:T(8,128)(2,1)} %pad_maximum_fusion), calls=%async_computation | async-start | bytes 4194304 | tf_op jit(solution)/shard_map/all_to_all | solution.py:158
  42.9 7.7 %slice-start.2 = ((s8[8388608]{0:T(1024)(128)(4,1)}), s8[4194304]{0:T(1024)(128)(4,1)S(1)}, s32[]{:S(2)}) async-start(s8[8388608]{0:T(1024)(128)(4,1)} %bitcast.154), calls=%async_computation.11 | async-start | bytes 8388608
  44.8 5.9 %slice-start.3 = ((s8[8388608]{0:T(1024)(128)(4,1)}), s8[4194304]{0:T(1024)(128)(4,1)S(1)}, s32[]{:S(2)}) async-start(s8[8388608]{0:T(1024)(128)(4,1)} %bitcast.154), calls=%async_computation.12 | async-start | bytes 8388608
  53.2 86.0 %copy-start.14 = (f32[1,32768]{1,0:T(1,128)S(1)}, f32[1,32768]{1,0:T(1,128)}, u32[]{:S(2)}) copy-start(f32[1,32768]{1,0:T(1,128)} %param.9) | copy-start | bytes 393220
  54.7 90.4 %copy-start.16 = (bf16[512,512,1]{1,0,2:T(8,128)(2,1)S(1)}, bf16[512,512,1]{1,0,2:T(8,128)(2,1)}, u32[]{:S(2)}) copy-start(bf16[512,512,1]{1,0,2:T(8,128)(2,1)} %constant.106) | copy-start | bytes 1572868
  76.4 68.7 %copy-start.8 = (bf16[16,2,128,256]{3,2,1,0:T(8,128)(2,1)}, bf16[16,2,128,256]{3,2,1,0:T(8,128)(2,1)S(1)}, u32[]{:S(2)}) copy-start(bf16[16,2,128,256]{3,2,1,0:T(8,128)(2,1)S(1)} %all-to-all-done) | copy-start | bytes 6291460
  76.4 78.8 %all-to-all-start.2 = ((bf16[16,2,128,256]{3,2,1,0:T(8,128)(2,1)}), bf16[16,2,128,256]{3,2,1,0:T(8,128)(2,1)}, u32[]{:S(2)}, u32[]{:S(2)}) async-start(bf16[16,2,128,256]{3,2,1,0:T(8,128)(2,1)} %pad_maximum_fusion.1), calls=%async_computation.2 | async-start | bytes 4194304 | tf_op jit(solution)/shard_map/all_to_all | solution.py:158
  148.7 3.3 copy-start.6
  148.7 3.1 copy-start.9
  155.2 59.7 %all-to-all-start.1 = ((bf16[16,2,128,256]{3,2,1,0:T(8,128)(2,1)}), bf16[16,2,128,256]{3,2,1,0:T(8,128)(2,1)}, u32[]{:S(2)}, u32[]{:S(2)}) async-start(bf16[16,2,128,256]{3,2,1,0:T(8,128)(2,1)} %bitcast.170), calls=%async_computation.1 | async-start | bytes 4194304 | tf_op jit(solution)/shard_map/all_to_all | solution.py:166
  166.4 79.7 %reduce-scatter.5.cloned.1.call-start = ((), (), s32[]{:S(2)}) async-start(), calls=%async_computation.6 | async-start | bytes 1114112 | tf_op jit(solution)/shard_map/reduce_scatter | solution.py:229
  166.7 5.4 %copy-start = (bf16[1,512,2,2048]{3,2,1,0:T(2,128)(2,1)S(1)}, bf16[1,512,2,2048]{3,2,1,0:T(2,128)(2,1)}, u32[]{:S(2)}) copy-start(bf16[1,512,2,2048]{3,2,1,0:T(2,128)(2,1)} %param.8) | copy-start | bytes 12582916
  174.5 3.4 copy-start.2
  178.8 3.5 copy-start.1
  182.2 5.4 %copy-start.3 = (bf16[64,8,2,2048]{3,1,2,0:T(8,128)(2,1)S(1)}, bf16[64,8,2,2048]{3,1,2,0:T(8,128)(2,1)}, u32[]{:S(2)}) copy-start(bf16[64,8,2,2048]{3,1,2,0:T(8,128)(2,1)} %copy-done.2) | copy-start | bytes 12582916
  209.0 2.8 copy-start.7
  214.9 94.5 %all-to-all-start.3 = ((bf16[16,2,128,256]{3,2,1,0:T(8,128)(2,1)}), bf16[16,2,128,256]{3,2,1,0:T(8,128)(2,1)}, u32[]{:S(2)}, u32[]{:S(2)}) async-start(bf16[16,2,128,256]{3,2,1,0:T(8,128)(2,1)} %bitcast.169), calls=%async_computation.3 | async-start | bytes 4194304 | tf_op jit(solution)/shard_map/all_to_all | solution.py:166
  222.7 125.6 %reduce-scatter.7.cloned.1.call-start = ((), (), s32[]{:S(2)}) async-start(), calls=%async_computation.8 | async-start | bytes 139264
  281.3 5.9 %copy-start.4 = (f32[256,2048]{1,0:T(8,128)S(1)}, f32[256,2048]{1,0:T(8,128)}, u32[]{:S(2)}) copy-start(f32[256,2048]{1,0:T(8,128)} %maximum_multiply_fusion) | copy-start | bytes 6291460
  289.9 154.9 %all-reduce.3.cloned.1.call-start = ((), (), s32[]{:S(2)}) async-start(), calls=%async_computation.7 | async-start | bytes 2097152 | tf_op jit(solution)/shard_map/psum | solution.py:276
  297.9 7.8 %slice-start.4 = ((s8[8388608]{0:T(1024)(128)(4,1)}), s8[4194304]{0:T(1024)(128)(4,1)S(1)}, s32[]{:S(2)}) async-start(s8[8388608]{0:T(1024)(128)(4,1)} %bitcast.156), calls=%async_computation.13 | async-start | bytes 8388608
  299.8 6.0 %slice-start.5 = ((s8[8388608]{0:T(1024)(128)(4,1)}), s8[4194304]{0:T(1024)(128)(4,1)S(1)}, s32[]{:S(2)}) async-start(s8[8388608]{0:T(1024)(128)(4,1)} %bitcast.156), calls=%async_computation.14 | async-start | bytes 8388608
  309.5 7.8 %slice-start.6 = ((s8[8388608]{0:T(1024)(128)(4,1)}), s8[4194304]{0:T(1024)(128)(4,1)S(1)}, s32[]{:S(2)}) async-start(s8[8388608]{0:T(1024)(128)(4,1)} %bitcast.158), calls=%async_computation.15 | async-start | bytes 8388608
  311.4 5.9 %slice-start.7 = ((s8[8388608]{0:T(1024)(128)(4,1)}), s8[4194304]{0:T(1024)(128)(4,1)S(1)}, s32[]{:S(2)}) async-start(s8[8388608]{0:T(1024)(128)(4,1)} %bitcast.158), calls=%async_computation.16 | async-start | bytes 8388608
  319.7 3.4 slice-start.8
  321.5 3.4 slice-start.9
  331.3 7.8 %copy-start.11 = (bf16[512,2048]{1,0:T(8,128)(2,1)S(1)}, bf16[512,2048]{1,0:T(8,128)(2,1)}, u32[]{:S(2)}) copy-start(bf16[512,2048]{1,0:T(8,128)(2,1)} %fusion.8) | copy-start | bytes 6291460
  339.1 7.5 %copy-start.12 = (bf16[512,2048]{1,0:T(8,128)(2,1)}, bf16[512,2048]{1,0:T(8,128)(2,1)S(1)}, u32[]{:S(2)}) copy-start(bf16[512,2048]{1,0:T(8,128)(2,1)S(1)} %get-tuple-element.12) | copy-start | bytes 6291460
  (2 other events, 4.9 us)
Sparse Core Ops, SparseCore 0:
  178.0 68.0 reduce-scatter.4
  290.0 57.8 reduce-scatter.6
  352.0 92.7 all-reduce.2

commit v2 on v1

--- a/solution.py
+++ b/solution.py
@@ -121,49 +121,68 @@
     return jnp.asarray(table.reshape(size, size).astype(np.float32), jnp.bfloat16)
 
 
-def plane_sum(psi, vloc, parts):
+def plane_out(psi, parts, plane_table):
     bands = psi.shape[1]
-    local_g = psi.shape[3]
-    side = NGRID * NGRID
-    planes = local_g // side
+    side = NGRID * NGRID
+    planes = psi.shape[3] // side
+    chunk = bands // CHUNKS
+    pieces = []
+    for first in range(0, bands, chunk):
+        part = psi[0, first : first + chunk].reshape(chunk, 2, planes, side)
+        part = part.transpose(2, 0, 1, 3).reshape(planes, chunk, 2 * side)
+        pieces.append(
+            jnp.stack(
+                [
+                    jnp.einsum(
+                        "qk,bk->qb", plane_table, part[p], preferred_element_type=jnp.float32
+                    )
+                    .astype(jnp.bfloat16)
+                    .reshape(parts, 2 * side // parts, chunk)
+                    for p in range(planes)
+                ],
+                1,
+            )
+        )
+    return pieces
+
+
+def exchange(piece):
+    return lax.all_to_all(piece, "ga", split_axis=0, concat_axis=0, tiled=True)
+
+
+def line_action(vloc, parts):
+    side = NGRID * NGRID
     points = side // parts
     group = min(8, points)
     groups = points // group
-    chunk = bands // CHUNKS
-    plane_table = plane_rotation()
     line_table = line_rotation(group)
     start = lax.axis_index("ga") * points
     own = lax.dynamic_slice_in_dim(vloc[0].reshape(NGRID, side), start, points, axis=1)
     own = own.reshape(NGRID, groups, group).transpose(1, 0, 2) * (1.0 / (NGRID * side))
     own = jnp.broadcast_to(own[..., None], (groups, NGRID, group, 2)).reshape(groups, -1, 1)
     scaled = (own * line_table.astype(jnp.float32)).astype(jnp.bfloat16)
-    action = jnp.einsum(
+    return jnp.einsum(
         "ea,gec->gac", line_table, scaled, preferred_element_type=jnp.float32
     ).astype(jnp.bfloat16)
+
+
+def line_step(action, lines):
+    parts, planes, rows, chunk = lines.shape
+    groups = action.shape[0]
+    lines = lines.reshape(parts * planes, groups, rows // groups, chunk)
+    lines = lines.transpose(1, 0, 2, 3).reshape(groups, -1, chunk)
+    lines = jnp.einsum(
+        "gac,gcb->gab", action, lines, preferred_element_type=jnp.float32
+    ).astype(jnp.bfloat16)
+    lines = lines.reshape(groups, parts * planes, rows // groups, chunk).transpose(1, 0, 2, 3)
+    return lines.reshape(parts, planes, rows, chunk)
+
+
+def plane_back(backs, plane_table):
+    side = NGRID * NGRID
     reals, imags = [], []
-    for first in range(0, bands, chunk):
-        part = psi[0, first : first + chunk].reshape(chunk, 2, planes, side)
-        part = part.transpose(2, 0, 1, 3).reshape(planes, chunk, 2 * side)
-        sent = jnp.stack(
-            [
-                jnp.einsum(
-                    "qk,bk->qb", plane_table, part[p], preferred_element_type=jnp.float32
-                )
-                .astype(jnp.bfloat16)
-                .reshape(parts, 2 * points, chunk)
-                for p in range(planes)
-            ],
-            1,
-        )
-        lines = lax.all_to_all(sent, "ga", split_axis=0, concat_axis=0, tiled=True)
-        lines = lines.reshape(parts * planes, groups, 2 * group, chunk)
-        lines = lines.transpose(1, 0, 2, 3).reshape(groups, -1, chunk)
-        lines = jnp.einsum(
-            "gac,gcb->gab", action, lines, preferred_element_type=jnp.float32
-        ).astype(jnp.bfloat16)
-        lines = lines.reshape(groups, parts * planes, 2 * group, chunk).transpose(1, 0, 2, 3)
-        lines = lines.reshape(parts, planes, 2 * points, chunk)
-        back = lax.all_to_all(lines, "ga", split_axis=0, concat_axis=0, tiled=True)
+    for back in backs:
+        chunk = back.shape[3]
         whole = [
             jnp.einsum(
                 "qb,qk->bk",
@@ -171,7 +190,7 @@
                 plane_table,
                 preferred_element_type=jnp.float32,
             )
-            for p in range(planes)
+            for p in range(back.shape[1])
         ]
         reals.append(jnp.concatenate([w[:, :side] for w in whole], 1))
         imags.append(jnp.concatenate([w[:, side:] for w in whole], 1))
@@ -202,8 +221,23 @@
     weight_float = weights.astype(jnp.float32)
     mixing = weight_float / jnp.sum(weight_float, axis=1, keepdims=True)
     centres = jnp.einsum("cj,jan->can", mixing, positions, precision=highest)
-    everyone = lax.all_gather(centres, "ga", axis=2, tiled=True)
     parts = lax.axis_size("ga")
+    near_oxygen = centres[0][:, 0::3]
+    own_waters = near_oxygen.shape[1]
+    everyone = lax.dynamic_update_slice(
+        jnp.zeros((3, own_waters * parts), jnp.float32),
+        near_oxygen,
+        (0, lax.axis_index("ga") * own_waters),
+    )
+    side = NGRID * NGRID
+    whole_planes = psi.shape[3] % side == 0 and side % parts == 0
+    if whole_planes:
+        plane_table = plane_rotation()
+        pieces = plane_out(psi, parts, plane_table)
+        pieces[-1], everyone = lax.optimization_barrier((pieces[-1], everyone))
+        lines = [exchange(piece) for piece in pieces]
+        action = line_action(vloc, parts)
+    oxygens = lax.psum(everyone, "ga")
     bands = psi.shape[1]
     local_g = psi.shape[3]
     flat_index = lax.axis_index("ga") * local_g + jnp.arange(local_g, dtype=jnp.int32)
@@ -217,28 +251,32 @@
     square = jnp.sum(gvectors * gvectors, axis=0)
     profile = jnp.exp(-0.5 * width_square * square)
     kinetic = 0.5 * square
-    oxygens = everyone[0][:, 0::3]
     wave_cos, wave_sin = waves(oxygens, gvectors, profile)
     table = jnp.concatenate(
         [jnp.concatenate([wave_cos, -wave_sin], 1), jnp.concatenate([wave_sin, wave_cos], 1)], 0
     ).astype(jnp.bfloat16)
     wavefunc = psi[0].reshape(bands, 2 * local_g)
-    real_part = wavefunc[:, :local_g]
-    imag_part = wavefunc[:, local_g:]
     partial_proj = (inner(table, wavefunc) * (1.0 / GVECS)).reshape(2, WATERS, bands)
     share = lax.psum_scatter(partial_proj, "ga", scatter_dimension=1, tiled=True).astype(
         jnp.bfloat16
     )
-    paired = jnp.concatenate([wavefunc, jnp.concatenate([imag_part, -real_part], 1)], 0).reshape(
-        2, bands, 2 * local_g
-    )
-    table_blocks = table.reshape(2, WATERS, 2 * local_g)
-    all_proj = lax.all_gather(share, "ga", axis=1, tiled=True)
+    table_blocks = table.reshape(2 * WATERS, 2 * local_g)
+    copies = jnp.broadcast_to(share[None], (parts,) + share.shape)
+    if whole_planes:
+        lines[-1], copies = lax.optimization_barrier((lines[-1], copies))
+    all_proj = lax.all_to_all(copies, "ga", split_axis=0, concat_axis=0, tiled=True)
+    if whole_planes:
+        moved = [line_step(action, line) for line in lines]
+        moved[0], all_proj = lax.optimization_barrier((moved[0], all_proj))
+        backs = [exchange(piece) for piece in moved]
+    all_proj = all_proj.transpose(1, 0, 2, 3).reshape(2 * WATERS, bands)
     nonlocal_term = jnp.einsum(
-        "kib,kig->bg", all_proj, table_blocks, preferred_element_type=jnp.float32
-    )
-    weighted = jnp.einsum("kib,kbg->ig", all_proj, paired, preferred_element_type=jnp.float32)
-    mixed_wave = wave_cos * weighted[:, local_g:] + wave_sin * weighted[:, :local_g]
+        "ib,ig->bg", all_proj, table_blocks, preferred_element_type=jnp.float32
+    )
+    crossed = jnp.dot(all_proj, wavefunc, preferred_element_type=jnp.float32)
+    weighted_re = crossed[:WATERS, :local_g] + crossed[WATERS:, local_g:]
+    weighted_im = crossed[:WATERS, local_g:] - crossed[WATERS:, :local_g]
+    mixed_wave = wave_cos * weighted_im + wave_sin * weighted_re
     force_part = (
         2.0
         * occupation
@@ -250,8 +288,8 @@
     hydrogen_zero = jnp.zeros_like(oxygen_force)
     dft_forces = [jnp.stack([oxygen_force, hydrogen_zero, hydrogen_zero], axis=2).reshape(3, -1)]
     wave_float = psi[0].astype(jnp.float32)
-    if local_g % (NGRID * NGRID) == 0 and (NGRID * NGRID) % parts == 0:
-        potential = plane_sum(psi, vloc, parts)
+    if whole_planes:
+        potential = plane_back(backs, plane_table)
     else:
         potential = grid_sum(psi, vloc, parts)
     hamil_re = (
@@ -264,23 +302,33 @@
         + potential[1]
         + nonlocal_strength * nonlocal_term[:, local_g:]
     )
-    trial = jnp.concatenate(
-        [wave_float[:, 0] - step_size * hamil_re, wave_float[:, 1] - step_size * hamil_im], 1
-    ).astype(jnp.bfloat16)
-    rotated = jnp.concatenate(
-        [trial, jnp.concatenate([-trial[:, local_g:], trial[:, :local_g]], 1)], 0
-    )
+    trial_re = (wave_float[:, 0] - step_size * hamil_re).astype(jnp.bfloat16)
+    trial_im = (wave_float[:, 1] - step_size * hamil_im).astype(jnp.bfloat16)
     row = lax.broadcasted_iota(jnp.int32, (bands, bands), 0)
     column = lax.broadcasted_iota(jnp.int32, (bands, bands), 1)
-    both = inner(trial, rotated) * (1.0 / GVECS)
-    packed = lax.psum(jnp.where(row <= column, both[:, :bands], both[:, bands:]), "ga")
-    turned = packed.T
-    even = jnp.where(row <= column, packed, turned)
-    odd = jnp.where(row > column, packed, jnp.where(row < column, -turned, 0.0))
-    identity = (row == column).astype(jnp.float32)
-    mixer = jnp.concatenate([1.5 * identity - 0.5 * even, -0.5 * odd], 1).astype(jnp.bfloat16)
-    updated = jnp.dot(mixer, rotated, preferred_element_type=jnp.float32)
-    new_waves = [updated.astype(jnp.bfloat16).reshape(bands, 2, local_g)]
+    even = inner(trial_re, trial_re) + inner(trial_im, trial_im)
+    odd = inner(trial_im, trial_re) - inner(trial_re, trial_im)
+    packed = jnp.where(row <= column, even, odd) * (1.0 / GVECS)
+    shares = lax.all_to_all(
+        packed.reshape(parts, bands // parts, bands), "ga", split_axis=0, concat_axis=0, tiled=True
+    )
+    own_rows = lax.broadcasted_iota(jnp.int32, (bands // parts, bands), 0) + lax.axis_index(
+        "ga"
+    ) * (bands // parts)
+    own_columns = lax.broadcasted_iota(jnp.int32, (bands // parts, bands), 1)
+    mixed_rows = jnp.where(own_rows == own_columns, 1.5, 0.0) - 0.5 * jnp.sum(shares, axis=0)
+    mixed = lax.all_gather(mixed_rows.astype(jnp.bfloat16), "ga", axis=0, tiled=True)
+    turned = mixed.T
+    mix_re = jnp.where(row <= column, mixed, turned)
+    mix_im = jnp.where(row > column, mixed, jnp.where(row < column, -turned, jnp.zeros_like(turned)))
+    both = jnp.concatenate([trial_re, trial_im], 0)
+    new_re = jnp.dot(
+        jnp.concatenate([mix_re, -mix_im], 1), both, preferred_element_type=jnp.float32
+    ).astype(jnp.bfloat16)
+    new_im = jnp.dot(
+        jnp.concatenate([mix_im, mix_re], 1), both, preferred_element_type=jnp.float32
+    ).astype(jnp.bfloat16)
+    new_waves = [jnp.stack([new_re, new_im], 1)]
     contracted_force = jnp.einsum("cj,can->jan", mixing, jnp.stack(dft_forces), precision=highest)
     bead_forces = near_forces + BEADS / CBEADS * contracted_force
     return (jnp.stack(new_waves), bead_forces)

time: 493 us -> 484 us (0.982)
  other arithmetic: 65.6 us -> 33.2 us
  waiting for transfers between devices: 139 us -> 169 us
  starting transfers between devices: 38.1 us -> 56.2 us
  matrix products: 90 us -> 74.8 us
  blocking collectives: 84.7 us -> 70.7 us
    psum x1 -> x0, waiting for transfers between devices: 94.7 us -> none  [per_device(): lax.psum(jnp.where(row <= column, both[:, :bands], both[:, bands:]), 'ga')]
    all_gather x2 -> x1, blocking collectives: 84.7 us -> 21.1 us  [per_device(): lax.all_gather(mixed_rows.astype(jnp.bfloat16), 'ga', axis=0, tiled=True)]
    unnamed x4 -> x3, waiting for transfers between devices: 0.07 us -> 56 us
    psum x0 -> x1, blocking collectives: none -> 49.6 us  [per_device(): oxygens = lax.psum(everyone, 'ga')]
    reduce_scatter x1, waiting for transfers between devices: 22.6 us -> 58.1 us  [per_device(): lax.psum_scatter(partial_proj, 'ga', scatter_dimension=1, tiled=True)]
    all_to_all x4 -> x6, waiting for transfers between devices: 21.7 us -> 54.7 us  [the longest x4 48.3 us: exchange(): return lax.all_to_all(piece, 'ga', split_axis=0, concat_axis=0, tiled=True)]
    concatenate x1 -> x0, other arithmetic: 21.4 us -> none  [per_device(): jnp.concatenate([wavefunc, jnp.concatenate([imag_part, -real_part], 1)], 0)]
    all_to_all x4 -> x6, starting transfers between devices: 37.6 us -> 56.1 us  [the longest x4 40.6 us: exchange(): return lax.all_to_all(piece, 'ga', split_axis=0, concat_axis=0, tiled=True)]
  transfers between devices with their start and end apart: 7 -> 8, of which waited for: 3 -> 5; matrix products, arithmetic and copies ran while one was open for 31% -> 19% of each run, Pallas kernels for 0% -> 0%
where the time goes in v2:
time: 484 us; the launch traced here: 476 us
  waiting for transfers between devices  169 us (35%)
  matrix products  74.8 us (15%)
  blocking collectives  70.7 us (15%)
  local copies, waits for them, and re-layouts  56.7 us (12%)
  starting transfers between devices  56.2 us (12%)
  other arithmetic  33.2 us (7%)
  between operations  15.4 us (3%)
    reduce_scatter x1, waiting for transfers between devices, per_device(): lax.psum_scatter(partial_proj, 'ga', scatter_dimension=1, tiled=True)  58.1 us
    unnamed x3, waiting for transfers between devices  56 us
    psum x1, blocking collectives, per_device(): oxygens = lax.psum(everyone, 'ga')  49.6 us
    all_to_all x4, waiting for transfers between devices, exchange(): return lax.all_to_all(piece, 'ga', split_axis=0, concat_axis=0, tiled=True)  48.3 us
    all_to_all x4, starting transfers between devices, exchange(): return lax.all_to_all(piece, 'ga', split_axis=0, concat_axis=0, tiled=True)  40.6 us
    unnamed x86, local copies, waits for them, and re-layouts  32.6 us
    all_gather x1, blocking collectives, per_device(): lax.all_gather(mixed_rows.astype(jnp.bfloat16), 'ga', axis=0, tiled=True)  21.1 us
    dot_general x4, matrix products, plane_out(): jnp.einsum('qk,bk->qb', plane_table, part[p], preferred_element_type=jnp....  16.7 us
  transfers between devices with their start and end apart: 8, of which 5 were waited for; matrix products, arithmetic and copies ran while one was open for 19% of the time, Pallas kernels for 0%

profile of v2, /device:TPU:0, one launch (start us, length us, event | category | flops | bytes accessed | tf_op | source)
XLA Modules:
  0.0 475.8 jit_solution(18000564476044155788)
XLA Ops:
  10.1 6.0 %fusion.67 = (bf16[1,256,2,2048]{3,2,1,0:T(2,128)(2,1)}, bf16[1,256,2,2048]{3,2,1,0:T(2,128)(2,1)}) fusion(bf16[1,512,2,2048]{3,2,1,0:T(2,128)(2,1)} %param.8), kind=kLoop, calls=%fused_computation.137 | loop fusion | bytes 8388608 | tf_op jit(solution)/shard_map/slice | solution.py:131
  16.2 4.7 copy.99
  21.0 5.9 %convolution_convert_fusion.3 = bf16[2048,256]{1,0:T(8,128)(2,1)S(1)} fusion(bf16[2048,2048]{1,0:T(8,128)(2,1)} %constant.102.clone, bf16[256,2048]{0,1:T(8,128)(2,1)S(1)} %bitcast.177), kind=kOutput, calls=%fused_computation.28 | convolution fusion | flops 2148007936 | bytes 10485760 | tf_op jit(solution)/shard_map/qk,bk->qb/dot_general | solution.py:136
  31.1 7.5 %all-to-all-start.1 = ((bf16[16,2,128,256]{3,2,1,0:T(8,128)(2,1)}), bf16[16,2,128,256]{3,2,1,0:T(8,128)(2,1)S(1)}, u32[]{:S(2)}, u32[]{:S(2)}) async-start(bf16[16,2,128,256]{3,2,1,0:T(8,128)(2,1)} %pad_maximum_fusion.4), calls=%async_computation.1 | async-start | bytes 4194304 | tf_op jit(solution)/shard_map/all_to_all | solution.py:150
  38.9 6.6 %copy.101 = bf16[64,8,2,2048]{3,1,2,0:T(8,128)(2,1)} copy(bf16[64,8,2,2048]{3,2,1,0:T(2,128)(2,1)} %bitcast.151) | data formatting | bytes 8388608
  45.5 6.1 %copy.98 = bf16[1,256,2,2048]{1,3,2,0:T(8,128)(2,1)} copy(bf16[1,256,2,2048]{3,2,1,0:T(2,128)(2,1)} %get-tuple-element.31) | data formatting | bytes 4194304
  51.6 49.6 %psum.7 = f32[256,3]{0,1:T(4,128)S(1)} all-reduce(f32[256,3]{0,1:T(4,128)S(1)} %bitcast.184), channel_id=1, replica_groups=mesh['rep'=2,'ga'=16] {'ga'}, use_global_device_ids=true, to_apply=%region_2.3 | all-reduce | flops 768 | bytes 6144 | tf_op jit(solution)/shard_map/psum | solution.py:240
  103.1 5.9 %convolution_convert_fusion.5 = bf16[2048,256]{1,0:T(8,128)(2,1)S(1)} fusion(bf16[2048,2048]{1,0:T(8,128)(2,1)} %constant.102.clone, bf16[256,2048]{0,1:T(8,128)(2,1)S(1)} %bitcast.178), kind=kOutput, calls=%fused_computation.30 | convolution fusion | flops 2148007936 | bytes 10485760 | tf_op jit(solution)/shard_map/qk,bk->qb/dot_general | solution.py:136
  113.2 7.6 %all-to-all-start = ((bf16[16,2,128,256]{3,2,1,0:T(8,128)(2,1)}), bf16[16,2,128,256]{3,2,1,0:T(8,128)(2,1)}, u32[]{:S(2)}, u32[]{:S(2)}) async-start(bf16[16,2,128,256]{3,2,1,0:T(8,128)(2,1)} %pad_maximum_fusion.3), calls=%async_computation | async-start | bytes 4194304 | tf_op jit(solution)/shard_map/all_to_all | solution.py:150
  121.5 4.2 multiply_add_fusion.1
  127.5 2.7 copy-done
  130.2 3.4 convolution_multiply_fusion
  135.2 58.1 %reduce-scatter.5.cloned.1.call-done = f32[2,16,512]{2,1,0:T(8,128)} async-done(((f32[2,256,512]{2,1,0:T(8,128)}), f32[2,16,512]{2,1,0:T(8,128)}) %reduce-scatter.5.cloned.1.call-update) | async-done | bytes 65552 | tf_op jit(solution)/shard_map/reduce_scatter | solution.py:260
  195.0 4.2 all-to-all-start.2
  199.8 3.7 fusion.13
  207.1 6.5 %all-to-all-done.2 = bf16[16,2,16,512]{3,2,1,0:T(8,128)(2,1)} async-done(((bf16[16,2,16,512]{3,2,1,0:T(8,128)(2,1)}), bf16[16,2,16,512]{3,2,1,0:T(8,128)(2,1)}, u32[]{:S(2)}, u32[]{:S(2)}) %all-to-all-start.2) | async-done | bytes 524320 | tf_op jit(solution)/shard_map/all_to_all | solution.py:267
  213.6 14.3 %all-to-all-start.4 = ((bf16[16,2,128,256]{3,2,1,0:T(8,128)(2,1)}), bf16[16,2,128,256]{3,2,1,0:T(8,128)(2,1)S(1)}, u32[]{:S(2)}, u32[]{:S(2)}) async-start(bf16[16,2,128,256]{3,2,1,0:T(8,128)(2,1)} %bitcast.156), calls=%async_computation.5 | async-start | bytes 4194304 | tf_op jit(solution)/shard_map/all_to_all | solution.py:150
  228.7 7.5 %bitcast_convert_fusion = f32[512,2,2048]{2,0,1:T(8,128)} fusion(bf16[1,512,2,2048]{3,2,1,0:T(2,128)(2,1)} %param.8), kind=kLoop, calls=%fused_computation.19 | loop fusion | flops 2097152 | bytes 12582912 | tf_op jit(solution)/shard_map/convert_element_type | solution.py:290
  242.2 26.6 %all-to-all-done.4 = bf16[16,2,128,256]{3,2,1,0:T(8,128)(2,1)S(1)} async-done(((bf16[16,2,128,256]{3,2,1,0:T(8,128)(2,1)}), bf16[16,2,128,256]{3,2,1,0:T(8,128)(2,1)S(1)}, u32[]{:S(2)}, u32[]{:S(2)}) %all-to-all-start.4) | async-done | bytes 2097184 | tf_op jit(solution)/shard_map/all_to_all | solution.py:150
  268.8 11.2 %all-to-all-start.3 = ((bf16[16,2,128,256]{3,2,1,0:T(8,128)(2,1)}), bf16[16,2,128,256]{3,2,1,0:T(8,128)(2,1)}, u32[]{:S(2)}, u32[]{:S(2)}) async-start(bf16[16,2,128,256]{3,2,1,0:T(8,128)(2,1)} %bitcast.155), calls=%async_computation.4 | async-start | bytes 4194304 | tf_op jit(solution)/shard_map/all_to_all | solution.py:150
  281.2 8.0 %fusion.25 = f32[512,4096]{1,0:T(8,128)} fusion(bf16[512,512]{1,0:T(8,128)(2,1)S(1)} %bitcast.167, bf16[256,2048]{1,0:T(8,128)(2,1)} %copy-done.20, bf16[256,2048]{1,0:T(8,128)(2,1)} %copy-done.19, bf16[256,2048]{1,0:T(8,128)(2,1)} %copy-done.18), kind=kOutput, calls=%fused_computation.52 | convolution fusion | flops 2164260864 | bytes 12058624 | tf_op jit(solution)/shard_map/ib,ig->bg/dot_general | solution.py:273
  289.5 5.9 %fusion.84 = f32[256,2048]{1,0:T(8,128)S(1)} fusion(bf16[2048,256]{1,0:T(8,128)(2,1)S(1)} %bitcast.165, bf16[2048,2048]{1,0:T(8,128)(2,1)} %constant.102.clone), kind=kOutput, calls=%fused_computation.154 | convolution fusion | flops 2147483648 | bytes 11534336 | tf_op jit(solution)/shard_map/qb,qk->bk/dot_general | solution.py:187
  299.4 21.6 %all-to-all-done.3 = bf16[16,2,128,256]{3,2,1,0:T(8,128)(2,1)} async-done(((bf16[16,2,128,256]{3,2,1,0:T(8,128)(2,1)}), bf16[16,2,128,256]{3,2,1,0:T(8,128)(2,1)}, u32[]{:S(2)}, u32[]{:S(2)}) %all-to-all-start.3) | async-done | bytes 2097184 | tf_op jit(solution)/shard_map/all_to_all | solution.py:150
  322.9 5.9 %fusion.82 = f32[256,2048]{1,0:T(8,128)S(1)} fusion(bf16[2048,256]{1,0:T(8,128)(2,1)S(1)} %bitcast.166, bf16[2048,2048]{1,0:T(8,128)(2,1)} %constant.102.clone), kind=kOutput, calls=%fused_computation.152 | convolution fusion | flops 2147483648 | bytes 11534336 | tf_op jit(solution)/shard_map/qb,qk->bk/dot_general | solution.py:187
  333.6 11.1 %fusion.8 = (bf16[512,2048]{1,0:T(8,128)(2,1)}, bf16[512,2048]{1,0:T(8,128)(2,1)}) fusion(f32[512,4096]{1,0:T(8,128)} %fusion.25, f32[256,1024]{1,0:T(8,128)S(1)} %get-tuple-element.40, f32[256,1024]{1,0:T(8,128)S(1)} %copy-done.9, f32[256,1024]{1,0:T(8,128)S(1)} %get-tuple-element.36, f32[256,1024]{1,0:T(8,128)} %get-tuple-element.34, ...), kind=kLoop, calls=%fused_computation.12 | loop fusion | flops 20971520 | bytes 29368320 | tf_op jit(solution)/shard_map/convert_element_type | solution.py:305
  344.7 3.7 fusion.85
  353.3 11.2 %all-to-all-start.5 = ((f32[16,32,512]{2,1,0:T(8,128)}), f32[16,32,512]{2,1,0:T(8,128)S(1)}, u32[]{:S(2)}, u32[]{:S(2)}) async-start(f32[16,32,512]{2,1,0:T(8,128)} %bitcast.169), calls=%async_computation.6 | async-start | bytes 2097152 | tf_op jit(solution)/shard_map/all_to_all | solution.py:312
  366.1 4.7 fusion.87
  374.8 56.0 %reduce-scatter.7.cloned.1.call-done = f32[16,3]{1,0:T(8,128)} async-done(((f32[256,3]{1,0:T(8,128)}), f32[16,3]{1,0:T(8,128)}) %reduce-scatter.7.cloned.1.call-update) | async-done | bytes 208
  433.7 21.1 %all_gather.3 = bf16[512,512]{1,0:T(8,128)(2,1)S(1)} all-gather(bf16[32,512]{1,0:T(8,128)(2,1)S(1)} %subtract_convert_fusion), channel_id=1, replica_groups=mesh['rep'=2,'ga'=16] {'ga'}, dimensions={0}, use_global_device_ids=true | all-gather | bytes 557056 | tf_op jit(solution)/shard_map/all_gather | solution.py:320
  455.3 4.1 fusion.11
  462.2 6.3 %copy.91 = bf16[1,512,2,2048]{3,2,1,0:T(2,128)(2,1)} copy(bf16[1,512,2,2048]{3,1,2,0:T(8,128)(2,1)S(1)} %maximum_bitcast_fusion) | data formatting | bytes 8388608
  (169 shorter events, 58.5 us)
Async XLA Ops:
  20.8 6.1 %slice-start = ((s8[8388608]{0:T(1024)(128)(4,1)}), s8[4194304]{0:T(1024)(128)(4,1)S(1)}, s32[]{:S(2)}) async-start(s8[8388608]{0:T(1024)(128)(4,1)} %bitcast.143), calls=%async_computation.10 | async-start | bytes 8388608
  21.0 5.9 %slice-start.1 = ((s8[8388608]{0:T(1024)(128)(4,1)}), s8[4194304]{0:T(1024)(128)(4,1)S(1)}, s32[]{:S(2)}) async-start(s8[8388608]{0:T(1024)(128)(4,1)} %bitcast.143), calls=%async_computation.11 | async-start | bytes 8388608
  31.1 82.2 %all-to-all-start.1 = ((bf16[16,2,128,256]{3,2,1,0:T(8,128)(2,1)}), bf16[16,2,128,256]{3,2,1,0:T(8,128)(2,1)S(1)}, u32[]{:S(2)}, u32[]{:S(2)}) async-start(bf16[16,2,128,256]{3,2,1,0:T(8,128)(2,1)} %pad_maximum_fusion.4), calls=%async_computation.1 | async-start | bytes 4194304 | tf_op jit(solution)/shard_map/all_to_all | solution.py:150
  38.6 62.6 %copy-start.22 = (f32[1,2048]{1,0:T(1,128)}, f32[1,2048]{1,0:T(1,128)S(1)}, u32[]{:S(2)}) copy-start(f32[1,2048]{1,0:T(1,128)S(1)} %fusion.52) | copy-start | bytes 24580
  38.8 62.4 %copy-start.24 = (f32[1,2048]{1,0:T(1,128)}, f32[1,2048]{1,0:T(1,128)S(1)}, u32[]{:S(2)}) copy-start(f32[1,2048]{1,0:T(1,128)S(1)} %get-tuple-element.84) | copy-start | bytes 24580
  101.3 7.8 %slice-start.2 = ((s8[8388608]{0:T(1024)(128)(4,1)}), s8[4194304]{0:T(1024)(128)(4,1)S(1)}, s32[]{:S(2)}) async-start(s8[8388608]{0:T(1024)(128)(4,1)} %bitcast.145), calls=%async_computation.12 | async-start | bytes 8388608
  103.1 5.9 %slice-start.3 = ((s8[8388608]{0:T(1024)(128)(4,1)}), s8[4194304]{0:T(1024)(128)(4,1)S(1)}, s32[]{:S(2)}) async-start(s8[8388608]{0:T(1024)(128)(4,1)} %bitcast.145), calls=%async_computation.13 | async-start | bytes 8388608
  111.6 10.0 %slice-start.8 = ((f32[1,2048]{1,0:T(1,128)}), f32[1,1024]{1,0:T(1,128)S(1)}, s32[]{:S(2)}) async-start(f32[1,2048]{1,0:T(1,128)} %copy-done.22), calls=%async_computation.18 | async-start | bytes 8192 | tf_op jit(solution)/shard_map/slice | solution.py:207
  113.2 81.8 %all-to-all-start = ((bf16[16,2,128,256]{3,2,1,0:T(8,128)(2,1)}), bf16[16,2,128,256]{3,2,1,0:T(8,128)(2,1)}, u32[]{:S(2)}, u32[]{:S(2)}) async-start(bf16[16,2,128,256]{3,2,1,0:T(8,128)(2,1)} %pad_maximum_fusion.3), calls=%async_computation | async-start | bytes 4194304 | tf_op jit(solution)/shard_map/all_to_all | solution.py:150
  120.8 72.5 %reduce-scatter.5.cloned.1.call-start = ((), (), s32[]{:S(2)}) async-start(), calls=%async_computation.8 | async-start | bytes 1114112 | tf_op jit(solution)/shard_map/reduce_scatter | solution.py:260
  121.5 5.9 %copy-start.26 = (f32[2048]{0:T(1024)}, f32[2048]{0:T(1024)S(1)}, u32[]{:S(2)}) copy-start(f32[2048]{0:T(1024)S(1)} %get-tuple-element.71) | copy-start | bytes 24580
  127.5 6.1 %copy-start.18 = (bf16[256,2048]{1,0:T(8,128)(2,1)}, bf16[256,2048]{1,0:T(8,128)(2,1)S(1)}, u32[]{:S(2)}) copy-start(bf16[256,2048]{1,0:T(8,128)(2,1)S(1)} %get-tuple-element.32) | copy-start | bytes 3145732
  127.5 6.1 %copy-start.19 = (bf16[256,2048]{1,0:T(8,128)(2,1)}, bf16[256,2048]{1,0:T(8,128)(2,1)S(1)}, u32[]{:S(2)}) copy-start(bf16[256,2048]{1,0:T(8,128)(2,1)S(1)} %get-tuple-element.33) | copy-start | bytes 3145732
  127.5 6.1 %copy-start.20 = (bf16[256,2048]{1,0:T(8,128)(2,1)}, bf16[256,2048]{1,0:T(8,128)(2,1)S(1)}, u32[]{:S(2)}) copy-start(bf16[256,2048]{1,0:T(8,128)(2,1)S(1)} %get-tuple-element.72) | copy-start | bytes 3145732
  195.0 18.5 %all-to-all-start.2 = ((bf16[16,2,16,512]{3,2,1,0:T(8,128)(2,1)}), bf16[16,2,16,512]{3,2,1,0:T(8,128)(2,1)}, u32[]{:S(2)}, u32[]{:S(2)}) async-start(bf16[16,2,16,512]{3,2,1,0:T(8,128)(2,1)} %broadcast_in_dim.18), calls=%async_computation.3 | async-start | bytes 1048576 | tf_op jit(solution)/shard_map/all_to_all | solution.py:267
  205.6 22.3 %copy-start.17 = (f32[32,3,48]{2,0,1:T(8,128)S(1)}, f32[32,3,48]{2,0,1:T(8,128)}, u32[]{:S(2)}) copy-start(f32[32,3,48]{2,0,1:T(8,128)} %param.6) | copy-start | bytes 55300
  213.6 55.2 %all-to-all-start.4 = ((bf16[16,2,128,256]{3,2,1,0:T(8,128)(2,1)}), bf16[16,2,128,256]{3,2,1,0:T(8,128)(2,1)S(1)}, u32[]{:S(2)}, u32[]{:S(2)}) async-start(bf16[16,2,128,256]{3,2,1,0:T(8,128)(2,1)} %bitcast.156), calls=%async_computation.5 | async-start | bytes 4194304 | tf_op jit(solution)/shard_map/all_to_all | solution.py:150
  268.8 52.3 %all-to-all-start.3 = ((bf16[16,2,128,256]{3,2,1,0:T(8,128)(2,1)}), bf16[16,2,128,256]{3,2,1,0:T(8,128)(2,1)}, u32[]{:S(2)}, u32[]{:S(2)}) async-start(bf16[16,2,128,256]{3,2,1,0:T(8,128)(2,1)} %bitcast.155), calls=%async_computation.4 | async-start | bytes 4194304 | tf_op jit(solution)/shard_map/all_to_all | solution.py:150
  281.2 8.1 %copy-start.11 = (bf16[16,2,16,512]{3,2,0,1:T(8,128)(2,1)}, bf16[16,2,16,512]{3,2,0,1:T(8,128)(2,1)S(1)}, u32[]{:S(2)}) copy-start(bf16[16,2,16,512]{3,2,0,1:T(8,128)(2,1)S(1)} %copy.82) | copy-start | bytes 1572868
  289.2 6.4 %slice-start.4 = ((s8[8388608]{0:T(1024)(128)(4,1)}), s8[4194304]{0:T(1024)(128)(4,1)S(1)}, s32[]{:S(2)}) async-start(s8[8388608]{0:T(1024)(128)(4,1)} %bitcast.147), calls=%async_computation.14 | async-start | bytes 8388608
  289.4 6.2 %slice-start.5 = ((s8[8388608]{0:T(1024)(128)(4,1)}), s8[4194304]{0:T(1024)(128)(4,1)S(1)}, s32[]{:S(2)}) async-start(s8[8388608]{0:T(1024)(128)(4,1)} %bitcast.147), calls=%async_computation.15 | async-start | bytes 8388608
  321.1 7.9 %slice-start.6 = ((s8[8388608]{0:T(1024)(128)(4,1)}), s8[4194304]{0:T(1024)(128)(4,1)S(1)}, s32[]{:S(2)}) async-start(s8[8388608]{0:T(1024)(128)(4,1)} %bitcast.149), calls=%async_computation.16 | async-start | bytes 8388608
  322.9 6.1 %slice-start.7 = ((s8[8388608]{0:T(1024)(128)(4,1)}), s8[4194304]{0:T(1024)(128)(4,1)S(1)}, s32[]{:S(2)}) async-start(s8[8388608]{0:T(1024)(128)(4,1)} %bitcast.149), calls=%async_computation.17 | async-start | bytes 8388608
  350.9 13.7 %copy-start.29 = (s32[1,32]{1,0:T(1,128)S(1)}, s32[1,32]{1,0:T(1,128)}, u32[]{:S(2)}) copy-start(s32[1,32]{1,0:T(1,128)} %param.7) | copy-start | bytes 388
  351.0 15.1 %copy-start.12 = (bf16[16,2,16,512]{3,2,0,1:T(8,128)(2,1)S(1)}, bf16[16,2,16,512]{3,2,0,1:T(8,128)(2,1)}, u32[]{:S(2)}) copy-start(bf16[16,2,16,512]{3,2,0,1:T(8,128)(2,1)} %copy-done.11) | copy-start | bytes 1572868
  353.3 80.3 %all-to-all-start.5 = ((f32[16,32,512]{2,1,0:T(8,128)}), f32[16,32,512]{2,1,0:T(8,128)S(1)}, u32[]{:S(2)}, u32[]{:S(2)}) async-start(f32[16,32,512]{2,1,0:T(8,128)} %bitcast.169), calls=%async_computation.6 | async-start | bytes 2097152 | tf_op jit(solution)/shard_map/all_to_all | solution.py:312
  364.5 66.3 %reduce-scatter.7.cloned.1.call-start = ((), (), s32[]{:S(2)}) async-start(), calls=%async_computation.9 | async-start | bytes 139264
  366.1 4.8 copy-start.8
  366.1 4.8 copy-start.23
  366.1 4.8 copy-start.25
  366.1 4.8 copy-start.27
  372.9 82.4 %copy-start.14 = (bf16[512,2048]{1,0:T(8,128)(2,1)S(1)}, bf16[512,2048]{1,0:T(8,128)(2,1)}, u32[]{:S(2)}) copy-start(bf16[512,2048]{1,0:T(8,128)(2,1)} %get-tuple-element.28) | copy-start | bytes 6291460
  (15 other events, 44.9 us)
Sparse Core Ops, SparseCore 0:
  133.7 59.5 reduce-scatter.4
  373.9 56.8 reduce-scatter.6

commit v3 on v2

--- a/solution.py
+++ b/solution.py
@@ -121,14 +121,14 @@
     return jnp.asarray(table.reshape(size, size).astype(np.float32), jnp.bfloat16)
 
 
-def plane_out(psi, parts, plane_table):
+def plane_out(psi, parts, plane_table, offset):
     bands = psi.shape[1]
     side = NGRID * NGRID
     planes = psi.shape[3] // side
     chunk = bands // CHUNKS
     pieces = []
     for first in range(0, bands, chunk):
-        part = psi[0, first : first + chunk].reshape(chunk, 2, planes, side)
+        part = lax.dynamic_slice_in_dim(psi[0], first + offset, chunk, axis=0).reshape(chunk, 2, planes, side)
         part = part.transpose(2, 0, 1, 3).reshape(planes, chunk, 2 * side)
         pieces.append(
             jnp.stack(
@@ -229,15 +229,14 @@
         near_oxygen,
         (0, lax.axis_index("ga") * own_waters),
     )
+    oxygens = lax.psum(everyone, "ga")
     side = NGRID * NGRID
     whole_planes = psi.shape[3] % side == 0 and side % parts == 0
     if whole_planes:
         plane_table = plane_rotation()
-        pieces = plane_out(psi, parts, plane_table)
-        pieces[-1], everyone = lax.optimization_barrier((pieces[-1], everyone))
+        pieces = plane_out(psi, parts, plane_table, (oxygens[0, 0] * 0.0).astype(jnp.int32))
         lines = [exchange(piece) for piece in pieces]
         action = line_action(vloc, parts)
-    oxygens = lax.psum(everyone, "ga")
     bands = psi.shape[1]
     local_g = psi.shape[3]
     flat_index = lax.axis_index("ga") * local_g + jnp.arange(local_g, dtype=jnp.int32)
@@ -284,9 +283,9 @@
         / GVECS
         * jnp.einsum("ag,ig->ai", gvectors, mixed_wave, precision=highest)
     )
-    oxygen_force = lax.psum_scatter(force_part, "ga", scatter_dimension=1, tiled=True)
-    hydrogen_zero = jnp.zeros_like(oxygen_force)
-    dft_forces = [jnp.stack([oxygen_force, hydrogen_zero, hydrogen_zero], axis=2).reshape(3, -1)]
+    force_rows = force_part.reshape(3, parts, own_waters).transpose(1, 0, 2)
+    force_rows = force_rows.reshape(parts, 1, 3 * own_waters)
+    force_rows = jnp.pad(force_rows, ((0, 0), (0, 0), (0, bands - 3 * own_waters)))
     wave_float = psi[0].astype(jnp.float32)
     if whole_planes:
         potential = plane_back(backs, plane_table)
@@ -310,13 +309,21 @@
     odd = inner(trial_im, trial_re) - inner(trial_re, trial_im)
     packed = jnp.where(row <= column, even, odd) * (1.0 / GVECS)
     shares = lax.all_to_all(
-        packed.reshape(parts, bands // parts, bands), "ga", split_axis=0, concat_axis=0, tiled=True
-    )
+        jnp.concatenate([packed.reshape(parts, bands // parts, bands), force_rows], 1),
+        "ga",
+        split_axis=0,
+        concat_axis=0,
+        tiled=True,
+    )
+    sums = jnp.sum(shares, axis=0)
+    oxygen_force = sums[-1, : 3 * own_waters].reshape(3, own_waters)
+    hydrogen_zero = jnp.zeros_like(oxygen_force)
+    dft_forces = [jnp.stack([oxygen_force, hydrogen_zero, hydrogen_zero], axis=2).reshape(3, -1)]
     own_rows = lax.broadcasted_iota(jnp.int32, (bands // parts, bands), 0) + lax.axis_index(
         "ga"
     ) * (bands // parts)
     own_columns = lax.broadcasted_iota(jnp.int32, (bands // parts, bands), 1)
-    mixed_rows = jnp.where(own_rows == own_columns, 1.5, 0.0) - 0.5 * jnp.sum(shares, axis=0)
+    mixed_rows = jnp.where(own_rows == own_columns, 1.5, 0.0) - 0.5 * sums[:-1]
     mixed = lax.all_gather(mixed_rows.astype(jnp.bfloat16), "ga", axis=0, tiled=True)
     turned = mixed.T
     mix_re = jnp.where(row <= column, mixed, turned)

time: 484 us -> 458 us (0.946)
  waiting for transfers between devices: 169 us -> 125 us
  local copies, waits for them, and re-layouts: 56.7 us -> 74.3 us
  matrix products: 74.8 us -> 87.9 us
  blocking collectives: 70.7 us -> 60.5 us
  starting transfers between devices: 56.2 us -> 47.6 us
  other arithmetic: 33.2 us -> 38.4 us
    unnamed x3 -> x1, waiting for transfers between devices: 56 us -> 0.02 us
    all_to_all x1, waiting for transfers between devices: 0.01 us -> 16.9 us  [per_device(): lax.all_to_all(jnp.concatenate([packed.reshape(parts, bands // parts, ban...]
    psum x1, blocking collectives: 49.6 us -> 35 us  [per_device(): oxygens = lax.psum(everyone, 'ga')]
    all_to_all x4, starting transfers between devices: 40.6 us -> 31.6 us  [exchange(): return lax.all_to_all(piece, 'ga', split_axis=0, concat_axis=0, tiled=True)]
    dot_general x4, matrix products: 16.7 us -> 25.8 us  [plane_out(): jnp.einsum('qk,bk->qb', plane_table, part[p], preferred_element_type=jnp....]
    dynamic_slice x0 -> x1, local copies, waits for them, and re-layouts: none -> 6.42 us  [plane_out(): lax.dynamic_slice_in_dim(psi[0], first + offset, chunk, axis=0)]
    unnamed x86 -> x69, local copies, waits for them, and re-layouts: 32.6 us -> 32.2 us
  transfers between devices with their start and end apart: 8 -> 7, of which waited for: 5 -> 6; matrix products, arithmetic and copies ran while one was open for 19% -> 24% of each run, Pallas kernels for 0% -> 0%
where the time goes in v3:
time: 458 us; the launch traced here: 450 us
  waiting for transfers between devices  125 us (27%)
  matrix products  87.9 us (19%)
  local copies, waits for them, and re-layouts  74.3 us (16%)
  blocking collectives  60.5 us (13%)
  starting transfers between devices  47.6 us (10%)
  other arithmetic  38.4 us (8%)
  between operations  15.8 us (3%)
    reduce_scatter x1, waiting for transfers between devices, per_device(): lax.psum_scatter(partial_proj, 'ga', scatter_dimension=1, tiled=True)  58.1 us
    all_to_all x4, waiting for transfers between devices, exchange(): return lax.all_to_all(piece, 'ga', split_axis=0, concat_axis=0, tiled=True)  46.6 us
    psum x1, blocking collectives, per_device(): oxygens = lax.psum(everyone, 'ga')  35 us
    unnamed x69, local copies, waits for them, and re-layouts  32.2 us
    all_to_all x4, starting transfers between devices, exchange(): return lax.all_to_all(piece, 'ga', split_axis=0, concat_axis=0, tiled=True)  31.6 us
    dot_general x4, matrix products, plane_out(): jnp.einsum('qk,bk->qb', plane_table, part[p], preferred_element_type=jnp....  25.8 us
    all_gather x1, blocking collectives, per_device(): lax.all_gather(mixed_rows.astype(jnp.bfloat16), 'ga', axis=0, tiled=True)  25.5 us
    all_to_all x1, waiting for transfers between devices, per_device(): lax.all_to_all(jnp.concatenate([packed.reshape(parts, bands // parts, ban...  16.9 us
  transfers between devices with their start and end apart: 7, of which 6 were waited for; matrix products, arithmetic and copies ran while one was open for 24% of the time, Pallas kernels for 0%

profile of v3, /device:TPU:0, one launch (start us, length us, event | category | flops | bytes accessed | tf_op | source)
XLA Modules:
  0.0 449.7 jit_solution(4897003384175119418)
XLA Ops:
  10.3 35.0 %psum.7 = f32[3,256]{1,0:T(4,128)S(1)} all-reduce(f32[3,256]{1,0:T(4,128)S(1)} %dynamic_update_slice.3), channel_id=1, replica_groups=mesh['rep'=2,'ga'=16] {'ga'}, use_global_device_ids=true, to_apply=%region_2.3 | all-reduce | flops 768 | bytes 6144 | tf_op jit(solution)/shard_map/psum | solution.py:232
  46.6 6.4 %constant_dynamic-slice_fusion = (bf16[1,256,2,2048]{3,2,1,0:T(2,128)(2,1)}, bf16[1,256,2,2048]{3,2,1,0:T(2,128)(2,1)S(1)}) fusion(bf16[1,512,2,2048]{3,2,1,0:T(2,128)(2,1)} %param.8, s32[]{:T(128)S(6)} %select_n.118, s32[]{:T(128)S(6)} %select_n.117), kind=kLoop, calls=%fused_computation.132 | loop fusion | bytes 8388616 | tf_op jit(solution)/shard_map/dynamic_slice | solution.py:131
  53.0 6.1 %copy.108 = bf16[1,256,2,2048]{1,3,2,0:T(8,128)(2,1)} copy(bf16[1,256,2,2048]{3,2,1,0:T(2,128)(2,1)} %get-tuple-element.26) | data formatting | bytes 4194304
  61.8 6.8 %fusion.16 = bf16[2048,256]{0,1:T(8,128)(2,1)} fusion(bf16[256,2048]{0,1:T(8,128)(2,1)S(1)} %bitcast.175, bf16[2048,2048]{1,0:T(8,128)(2,1)} %constant.111.clone), kind=kOutput, calls=%fused_computation.33 | convolution fusion | flops 2148007936 | bytes 10485760 | tf_op jit(solution)/shard_map/qk,bk->qb/dot_general | solution.py:136
  70.0 7.1 %fusion.17 = bf16[2048,256]{0,1:T(8,128)(2,1)} fusion(bf16[256,2048]{0,1:T(8,128)(2,1)} %bitcast.173, bf16[2048,2048]{1,0:T(8,128)(2,1)} %constant.111.clone), kind=kOutput, calls=%fused_computation.34 | convolution fusion | flops 2148007936 | bytes 10485760 | tf_op jit(solution)/shard_map/qk,bk->qb/dot_general | solution.py:136
  82.2 4.7 %all-to-all-start.1 = ((bf16[16,2,128,256]{3,2,1,0:T(8,128)(2,1)}), bf16[16,2,128,256]{3,2,1,0:T(8,128)(2,1)}, u32[]{:S(2)}, u32[]{:S(2)}) async-start(bf16[16,2,128,256]{3,2,1,0:T(8,128)(2,1)} %pad_maximum_fusion.4), calls=%async_computation.1 | async-start | bytes 4194304 | tf_op jit(solution)/shard_map/all_to_all | solution.py:150
  87.1 4.1 copy.107
  93.9 5.8 %fusion.14 = bf16[2048,256]{0,1:T(8,128)(2,1)S(1)} fusion(bf16[256,2048]{0,1:T(8,128)(2,1)S(1)} %bitcast.176, bf16[2048,2048]{1,0:T(8,128)(2,1)} %constant.111.clone), kind=kOutput, calls=%fused_computation.31 | convolution fusion | flops 2148007936 | bytes 10485760 | tf_op jit(solution)/shard_map/qk,bk->qb/dot_general | solution.py:136
  100.2 6.1 %fusion.15 = bf16[2048,256]{0,1:T(8,128)(2,1)S(1)} fusion(bf16[256,2048]{0,1:T(8,128)(2,1)} %bitcast.174, bf16[2048,2048]{1,0:T(8,128)(2,1)} %constant.111.clone), kind=kOutput, calls=%fused_computation.32 | convolution fusion | flops 2148007936 | bytes 10485760 | tf_op jit(solution)/shard_map/qk,bk->qb/dot_general | solution.py:136
  106.8 6.6 %copy.111 = bf16[64,8,2,2048]{3,1,2,0:T(8,128)(2,1)} copy(bf16[64,8,2,2048]{3,2,1,0:T(2,128)(2,1)} %bitcast.149) | data formatting | bytes 8388608
  115.1 12.7 %all-to-all-done.1 = bf16[16,2,128,256]{3,2,1,0:T(8,128)(2,1)} async-done(((bf16[16,2,128,256]{3,2,1,0:T(8,128)(2,1)}), bf16[16,2,128,256]{3,2,1,0:T(8,128)(2,1)}, u32[]{:S(2)}, u32[]{:S(2)}) %all-to-all-start.1) | async-done | bytes 2097184 | tf_op jit(solution)/shard_map/all_to_all | solution.py:150
  127.8 11.2 %all-to-all-start = ((bf16[16,2,128,256]{3,2,1,0:T(8,128)(2,1)}), bf16[16,2,128,256]{3,2,1,0:T(8,128)(2,1)S(1)}, u32[]{:S(2)}, u32[]{:S(2)}) async-start(bf16[16,2,128,256]{3,2,1,0:T(8,128)(2,1)} %pad_maximum_fusion.3), calls=%async_computation | async-start | bytes 4194304 | tf_op jit(solution)/shard_map/all_to_all | solution.py:150
  140.1 4.2 multiply_add_fusion.1
  153.7 58.1 %reduce-scatter.2.cloned.1.call-done = f32[2,16,512]{2,1,0:T(8,128)} async-done(((f32[2,256,512]{2,1,0:T(8,128)}), f32[2,16,512]{2,1,0:T(8,128)}) %reduce-scatter.2.cloned.1.call-update) | async-done | bytes 65552 | tf_op jit(solution)/shard_map/reduce_scatter | solution.py:259
  213.5 4.2 all-to-all-start.2
  218.2 3.7 fusion.13
  232.0 4.6 %all-to-all-start.4 = ((bf16[16,2,128,256]{3,2,1,0:T(8,128)(2,1)}), bf16[16,2,128,256]{3,2,1,0:T(8,128)(2,1)}, u32[]{:S(2)}, u32[]{:S(2)}) async-start(bf16[16,2,128,256]{3,2,1,0:T(8,128)(2,1)} %bitcast.153), calls=%async_computation.5 | async-start | bytes 4194304 | tf_op jit(solution)/shard_map/all_to_all | solution.py:150
  236.6 7.5 %bitcast_convert_fusion = f32[512,2,2048]{2,0,1:T(8,128)} fusion(bf16[1,512,2,2048]{3,2,1,0:T(2,128)(2,1)} %param.8), kind=kLoop, calls=%fused_computation.19 | loop fusion | flops 2097152 | bytes 12582912 | tf_op jit(solution)/shard_map/convert_element_type | solution.py:289
  251.7 5.6 %fusion.92 = f32[512,4096]{1,0:T(8,128)} fusion(bf16[512,512]{1,0:T(8,128)(2,1)S(1)} %bitcast.168, bf16[512,4096]{1,0:T(8,128)(2,1)S(1)} %bitcast.151), kind=kOutput, calls=%fused_computation.168 | convolution fusion | flops 2147483648 | bytes 13107200 | tf_op jit(solution)/shard_map/dot_general | solution.py:275
  257.4 20.3 %all-to-all-done.4 = bf16[16,2,128,256]{3,2,1,0:T(8,128)(2,1)} async-done(((bf16[16,2,128,256]{3,2,1,0:T(8,128)(2,1)}), bf16[16,2,128,256]{3,2,1,0:T(8,128)(2,1)}, u32[]{:S(2)}, u32[]{:S(2)}) %all-to-all-start.4) | async-done | bytes 2097184 | tf_op jit(solution)/shard_map/all_to_all | solution.py:150
  277.6 11.2 %all-to-all-start.3 = ((bf16[16,2,128,256]{3,2,1,0:T(8,128)(2,1)}), bf16[16,2,128,256]{3,2,1,0:T(8,128)(2,1)S(1)}, u32[]{:S(2)}, u32[]{:S(2)}) async-start(bf16[16,2,128,256]{3,2,1,0:T(8,128)(2,1)} %bitcast.24), calls=%async_computation.4 | async-start | bytes 4194304 | tf_op jit(solution)/shard_map/all_to_all | solution.py:150
  288.8 6.3 %fusion.30 = f32[3,256]{1,0:T(4,128)S(1)} fusion(f32[512,4096]{1,0:T(8,128)} %fusion.92, f32[256,1024]{1,0:T(8,128)} %copy-done.5, f32[256,1024]{1,0:T(8,128)} %copy-done.4, f32[256,1024]{1,0:T(8,128)} %copy-done.6, f32[256,1024]{1,0:T(8,128)S(1)} %get-tuple-element.60, f32[2048]{0:T(1024)S(1)} %copy-done.24, f32[1,2048]{1,0:T(1,128)S(1)} %copy-done.20, ...), kind=kOutput, calls=%fused_computation.59 | convolution fusion | flops 23606016 | bytes 12618752 | tf_op jit(solution)/shard_map/ag,ig->ai/dot_general | solution.py:284
  295.4 8.0 %fusion.29 = f32[512,4096]{1,0:T(8,128)} fusion(bf16[512,512]{1,0:T(8,128)(2,1)} %bitcast.169, bf16[256,2048]{1,0:T(8,128)(2,1)} %copy-done.17, bf16[256,2048]{1,0:T(8,128)(2,1)} %copy-done.16, bf16[256,2048]{1,0:T(8,128)(2,1)} %copy-done.15), kind=kOutput, calls=%fused_computation.58 | convolution fusion | flops 2164260864 | bytes 12058624 | tf_op jit(solution)/shard_map/ib,ig->bg/dot_general | solution.py:272
  305.2 5.9 %fusion.89 = f32[256,2048]{1,0:T(8,128)S(1)} fusion(bf16[2048,256]{1,0:T(8,128)(2,1)S(1)} %bitcast.162, bf16[2048,2048]{1,0:T(8,128)(2,1)} %constant.111.clone), kind=kOutput, calls=%fused_computation.165 | convolution fusion | flops 2147483648 | bytes 11534336 | tf_op jit(solution)/shard_map/qb,qk->bk/dot_general | solution.py:187
  316.1 13.7 %all-to-all-done.3 = bf16[16,2,128,256]{3,2,1,0:T(8,128)(2,1)S(1)} async-done(((bf16[16,2,128,256]{3,2,1,0:T(8,128)(2,1)}), bf16[16,2,128,256]{3,2,1,0:T(8,128)(2,1)S(1)}, u32[]{:S(2)}, u32[]{:S(2)}) %all-to-all-start.3) | async-done | bytes 2097184 | tf_op jit(solution)/shard_map/all_to_all | solution.py:150
  330.0 5.9 %fusion.87 = f32[256,2048]{1,0:T(8,128)S(1)} fusion(bf16[2048,256]{1,0:T(8,128)(2,1)S(1)} %bitcast.163, bf16[2048,2048]{1,0:T(8,128)(2,1)} %constant.111.clone), kind=kOutput, calls=%fused_computation.163 | convolution fusion | flops 2147483648 | bytes 11534336 | tf_op jit(solution)/shard_map/qb,qk->bk/dot_general | solution.py:187
  340.7 10.8 %fusion.8 = (bf16[512,2048]{1,0:T(8,128)(2,1)}, bf16[512,2048]{1,0:T(8,128)(2,1)}) fusion(f32[512,4096]{1,0:T(8,128)} %fusion.29, f32[256,1024]{1,0:T(8,128)S(1)} %get-tuple-element.36, f32[256,1024]{1,0:T(8,128)S(1)} %copy-done.8, f32[256,1024]{1,0:T(8,128)S(1)} %get-tuple-element.32, f32[256,1024]{1,0:T(8,128)S(1)} %get-tuple-element.30, ...), kind=kLoop, calls=%fused_computation.12 | loop fusion | flops 20971520 | bytes 29368320 | tf_op jit(solution)/shard_map/convert_element_type | solution.py:304
  360.3 11.2 %all-to-all-start.5 = ((f32[16,33,512]{2,1,0:T(8,128)}), f32[16,33,512]{2,1,0:T(8,128)S(1)}, u32[]{:S(2)}, u32[]{:S(2)}) async-start(f32[16,33,512]{2,1,0:T(8,128)} %select_maximum_fusion), calls=%async_computation.6 | async-start | bytes 2621440 | tf_op jit(solution)/shard_map/all_to_all | solution.py:311
  381.9 16.9 %all-to-all-done.5 = f32[16,33,512]{2,1,0:T(8,128)S(1)} async-done(((f32[16,33,512]{2,1,0:T(8,128)}), f32[16,33,512]{2,1,0:T(8,128)S(1)}, u32[]{:S(2)}, u32[]{:S(2)}) %all-to-all-start.5) | async-done | bytes 1081376 | tf_op jit(solution)/shard_map/all_to_all | solution.py:311
  403.2 25.5 %all_gather.3 = bf16[512,512]{1,0:T(8,128)(2,1)S(1)} all-gather(bf16[32,512]{1,0:T(8,128)(2,1)S(1)} %fusion.51), channel_id=1, replica_groups=mesh['rep'=2,'ga'=16] {'ga'}, dimensions={0}, use_global_device_ids=true | all-gather | bytes 557056 | tf_op jit(solution)/shard_map/all_gather | solution.py:327
  429.2 4.1 fusion.11
  436.1 6.3 %copy.98 = bf16[1,512,2,2048]{3,2,1,0:T(2,128)(2,1)} copy(bf16[1,512,2,2048]{3,1,2,0:T(8,128)(2,1)S(1)} %maximum_bitcast_fusion) | data formatting | bytes 8388608
  (158 shorter events, 87.4 us)
Async XLA Ops:
  82.2 45.6 %all-to-all-start.1 = ((bf16[16,2,128,256]{3,2,1,0:T(8,128)(2,1)}), bf16[16,2,128,256]{3,2,1,0:T(8,128)(2,1)}, u32[]{:S(2)}, u32[]{:S(2)}) async-start(bf16[16,2,128,256]{3,2,1,0:T(8,128)(2,1)} %pad_maximum_fusion.4), calls=%async_computation.1 | async-start | bytes 4194304 | tf_op jit(solution)/shard_map/all_to_all | solution.py:150
  86.9 26.5 %copy-start.19 = (f32[1,2048]{1,0:T(1,128)}, f32[1,2048]{1,0:T(1,128)S(1)}, u32[]{:S(2)}) copy-start(f32[1,2048]{1,0:T(1,128)S(1)} %fusion.58) | copy-start | bytes 24580
  87.0 26.4 %copy-start.21 = (f32[1,2048]{1,0:T(1,128)}, f32[1,2048]{1,0:T(1,128)S(1)}, u32[]{:S(2)}) copy-start(f32[1,2048]{1,0:T(1,128)S(1)} %get-tuple-element.80) | copy-start | bytes 24580
  113.5 26.6 %slice-start.4 = ((f32[1,2048]{1,0:T(1,128)}), f32[1,1024]{1,0:T(1,128)S(1)}, s32[]{:S(2)}) async-start(f32[1,2048]{1,0:T(1,128)} %copy-done.19), calls=%async_computation.12 | async-start | bytes 8192 | tf_op jit(solution)/shard_map/slice | solution.py:207
  127.8 85.7 %all-to-all-start = ((bf16[16,2,128,256]{3,2,1,0:T(8,128)(2,1)}), bf16[16,2,128,256]{3,2,1,0:T(8,128)(2,1)S(1)}, u32[]{:S(2)}, u32[]{:S(2)}) async-start(bf16[16,2,128,256]{3,2,1,0:T(8,128)(2,1)} %pad_maximum_fusion.3), calls=%async_computation | async-start | bytes 4194304 | tf_op jit(solution)/shard_map/all_to_all | solution.py:150
  139.0 72.8 %reduce-scatter.2.cloned.1.call-start = ((), (), s32[]{:S(2)}) async-start(), calls=%async_computation.7 | async-start | bytes 1114112 | tf_op jit(solution)/shard_map/reduce_scatter | solution.py:259
  140.1 5.9 %copy-start.23 = (f32[2048]{0:T(1024)}, f32[2048]{0:T(1024)S(1)}, u32[]{:S(2)}) copy-start(f32[2048]{0:T(1024)S(1)} %get-tuple-element.67) | copy-start | bytes 24580
  144.3 4.5 copy-start
  146.0 6.2 %copy-start.15 = (bf16[256,2048]{1,0:T(8,128)(2,1)}, bf16[256,2048]{1,0:T(8,128)(2,1)S(1)}, u32[]{:S(2)}) copy-start(bf16[256,2048]{1,0:T(8,128)(2,1)S(1)} %get-tuple-element.28) | copy-start | bytes 3145732
  146.0 6.1 %copy-start.16 = (bf16[256,2048]{1,0:T(8,128)(2,1)}, bf16[256,2048]{1,0:T(8,128)(2,1)S(1)}, u32[]{:S(2)}) copy-start(bf16[256,2048]{1,0:T(8,128)(2,1)S(1)} %get-tuple-element.29) | copy-start | bytes 3145732
  146.0 6.1 %copy-start.17 = (bf16[256,2048]{1,0:T(8,128)(2,1)}, bf16[256,2048]{1,0:T(8,128)(2,1)S(1)}, u32[]{:S(2)}) copy-start(bf16[256,2048]{1,0:T(8,128)(2,1)S(1)} %get-tuple-element.68) | copy-start | bytes 3145732
  148.8 4.0 copy-start.18
  213.5 18.5 %all-to-all-start.2 = ((bf16[16,2,16,512]{3,2,1,0:T(8,128)(2,1)}), bf16[16,2,16,512]{3,2,1,0:T(8,128)(2,1)}, u32[]{:S(2)}, u32[]{:S(2)}) async-start(bf16[16,2,16,512]{3,2,1,0:T(8,128)(2,1)} %broadcast_in_dim.18), calls=%async_computation.3 | async-start | bytes 1048576 | tf_op jit(solution)/shard_map/all_to_all | solution.py:266
  222.0 4.8 %copy-start.2 = (bf16[8,512,512]{2,1,0:T(8,128)(2,1)}, bf16[8,512,512]{2,1,0:T(8,128)(2,1)S(1)}, u32[]{:S(2)}) copy-start(bf16[8,512,512]{2,1,0:T(8,128)(2,1)S(1)} %fusion.13) | copy-start | bytes 12582916
  232.0 45.6 %all-to-all-start.4 = ((bf16[16,2,128,256]{3,2,1,0:T(8,128)(2,1)}), bf16[16,2,128,256]{3,2,1,0:T(8,128)(2,1)}, u32[]{:S(2)}, u32[]{:S(2)}) async-start(bf16[16,2,128,256]{3,2,1,0:T(8,128)(2,1)} %bitcast.153), calls=%async_computation.5 | async-start | bytes 4194304 | tf_op jit(solution)/shard_map/all_to_all | solution.py:150
  247.9 3.9 copy-start.1
  257.3 31.5 %copy-start.20 = (f32[1,2048]{1,0:T(1,128)S(1)}, f32[1,2048]{1,0:T(1,128)}, u32[]{:S(2)}) copy-start(f32[1,2048]{1,0:T(1,128)} %copy-done.19) | copy-start | bytes 24580
  257.4 31.5 %copy-start.22 = (f32[1,2048]{1,0:T(1,128)S(1)}, f32[1,2048]{1,0:T(1,128)}, u32[]{:S(2)}) copy-start(f32[1,2048]{1,0:T(1,128)} %copy-done.21) | copy-start | bytes 24580
  257.4 31.5 %copy-start.24 = (f32[2048]{0:T(1024)S(1)}, f32[2048]{0:T(1024)}, u32[]{:S(2)}) copy-start(f32[2048]{0:T(1024)} %copy-done.23) | copy-start | bytes 24580
  277.6 52.2 %all-to-all-start.3 = ((bf16[16,2,128,256]{3,2,1,0:T(8,128)(2,1)}), bf16[16,2,128,256]{3,2,1,0:T(8,128)(2,1)S(1)}, u32[]{:S(2)}, u32[]{:S(2)}) async-start(bf16[16,2,128,256]{3,2,1,0:T(8,128)(2,1)} %bitcast.24), calls=%async_computation.4 | async-start | bytes 4194304 | tf_op jit(solution)/shard_map/all_to_all | solution.py:150
  303.3 8.9 %slice-start = ((s8[8388608]{0:T(1024)(128)(4,1)}), s8[4194304]{0:T(1024)(128)(4,1)S(1)}, s32[]{:S(2)}) async-start(s8[8388608]{0:T(1024)(128)(4,1)} %bitcast.145), calls=%async_computation.8 | async-start | bytes 8388608
  305.2 7.1 %slice-start.1 = ((s8[8388608]{0:T(1024)(128)(4,1)}), s8[4194304]{0:T(1024)(128)(4,1)S(1)}, s32[]{:S(2)}) async-start(s8[8388608]{0:T(1024)(128)(4,1)} %bitcast.145), calls=%async_computation.9 | async-start | bytes 8388608
  329.8 6.3 %slice-start.2 = ((s8[8388608]{0:T(1024)(128)(4,1)}), s8[4194304]{0:T(1024)(128)(4,1)S(1)}, s32[]{:S(2)}) async-start(s8[8388608]{0:T(1024)(128)(4,1)} %bitcast.147), calls=%async_computation.10 | async-start | bytes 8388608
  330.0 6.1 %slice-start.3 = ((s8[8388608]{0:T(1024)(128)(4,1)}), s8[4194304]{0:T(1024)(128)(4,1)S(1)}, s32[]{:S(2)}) async-start(s8[8388608]{0:T(1024)(128)(4,1)} %bitcast.147), calls=%async_computation.11 | async-start | bytes 8388608
  338.5 2.2 copy-start.9
  338.5 2.2 copy-start.25
  351.5 3.7 copy-start.11
  351.5 3.7 copy-start.12
  359.1 12.5 %copy-start.14 = (f32[32,3,48]{2,0,1:T(8,128)S(1)}, f32[32,3,48]{2,0,1:T(8,128)}, u32[]{:S(2)}) copy-start(f32[32,3,48]{2,0,1:T(8,128)} %param.6) | copy-start | bytes 55300
  359.1 21.5 %copy-start.26 = (s32[1,32]{1,0:T(1,128)S(1)}, s32[1,32]{1,0:T(1,128)}, u32[]{:S(2)}) copy-start(s32[1,32]{1,0:T(1,128)} %param.7) | copy-start | bytes 388
  360.3 38.5 %all-to-all-start.5 = ((f32[16,33,512]{2,1,0:T(8,128)}), f32[16,33,512]{2,1,0:T(8,128)S(1)}, u32[]{:S(2)}, u32[]{:S(2)}) async-start(f32[16,33,512]{2,1,0:T(8,128)} %select_maximum_fusion), calls=%async_computation.6 | async-start | bytes 2621440 | tf_op jit(solution)/shard_map/all_to_all | solution.py:311
  429.2 4.2 copy-start.13
  (7 other events, 10.7 us)
Sparse Core Ops, SparseCore 0:
  152.3 59.4 reduce-scatter.1
